TPU v7x, 256 devices: a whole 4x4x8 slice. The times are simulated.
256 devices in a mesh: band: 2 (over core), grow: 8 (over z), gcol: 16 (over y, x).
Axes of the slice: x: 4, y: 4, z: 8, core: 2. Of those that a mesh axis runs over, the one named last changes fastest.
Arguments:
- valence_orbitals: bfloat16 [16, 98304], replicated, may hold values from -6 to 6
- conduction_orbitals: bfloat16 [1024, 98304], P(('band', 'grow', 'gcol')), may hold values from -6 to 6
- valence_energy: float32 [16], replicated, may hold values from -3 to -0.5
- conduction_energy: float32 [1024], replicated, may hold values from 0.5 to 3
- coulomb_root: float32 [12288], replicated, may hold values from 0.2 to 2
- pair_bands: int32 [2, 5120], P(None, ('band', 'grow', 'gcol')), may hold values from 0 to 1023, as said below
- slot_counts: int32 [256], P(('band', 'grow', 'gcol')), may hold values from 1 to 19, as said below
Outputs:
- chi_zero: float32 [2, 12288, 12288], P('band', 'grow', 'gcol')
Inputs may be any that keep to these rules, and one draw needn't show every extreme that they name: `pair_bands`: the slots of device d name conduction orbitals d * 4 to (d + 1) * 4 - 1 only, each of them at least once; no (valence, conduction) pair appears in two slots anywhere. `slot_counts`: the two devices of one chip (same grow and gcol index, band 0 and band 1) hold at most 20 live slots together; some chip holds exactly 20, and some device holds exactly 19.
All inputs are finite; a program needn't handle non-finite values.
Results may differ from a plain program's by a relative error of at most 0.012.
Values may be sent and summed in bfloat16 or wider, within the bound.
No kernel may reach another device: no remote copies, remote signals or barrier semaphores. Data moves between devices by JAX's collectives and lax.ppermute only.
A program may use at most 128 MiB of HBM per device.

v0:
```python
import math

import jax
import jax.numpy as jnp
import numpy as np
from jax import lax
from jax.experimental import pallas as pl
from jax.experimental.pallas import tpu as pltpu
from jax.sharding import Mesh
from jax.sharding import PartitionSpec as P


N1, N2, N3 = 16, 24, 32
M1, M2, M3 = 32, 48, 64
NP = N2 * N3
KP = M2 * M3
MG = M1 * KP
ROW = 2 * NP
TOTAL = 5120
SLOTS = 20
HALF = 10
GROW, GCOL = 8, 16
LANES = 128
CHUNKS = KP // LANES
LINES = MG // LANES + 4
PANEL = GROW * GCOL * HALF
BLOCK = 64
ROWBLOCK = 120
COLROWS = GCOL * BLOCK + 4
WIDTH = NP // LANES
STEP = 512
ZAROUND = (0, 7, 6, 5, 4, 1, 2, 3)
F32, BF16 = jnp.float32, jnp.bfloat16
VMEM = pltpu.VMEM
SMEM = pltpu.SMEM


def wave_table(keep, length):
    wave = (np.arange(keep)[:, None] - keep // 2) % length
    angles = 2.0 * np.pi * (wave * np.arange(length)[None, :] % length) / length
    return np.cos(angles) + np.sin(angles)


def halves(table):
    high = table.astype(np.float32).astype(BF16)
    return high, (table - high.astype(np.float64)).astype(np.float32).astype(BF16)


def tables():
    second = np.repeat(wave_table(N2, M2).T, N3, axis=1)
    third = np.tile(wave_table(N3, M3).T, (1, N2))
    first = wave_table(N1, M1)
    mixed = np.zeros((N1, 16, HALF, M1))
    for p in range(HALF):
        mixed[:, p, p] = first
    return (
        second.astype(np.float32),
        third.astype(np.float32),
        halves(mixed.reshape(N1 * 16, HALF * M1)),
    )


def density_kernel(
    place, mine, other, val_e, con_e, val, con_mine, con_other, scale, second, third, mix_hi, mix_lo,
    *refs,
):
    col_out, row_out, vals, cons, lhs, acc, table, done, lines, row_lines = refs
    band = place[0] >> 7

    def spread(a, carry):
        for t in range(CHUNKS):
            where = pl.ds(pl.multiple_of(a * KP + t * LANES, LANES), LANES)
            line = t * M1 + a
            vals[pl.ds(line, 16, stride=LINES), :] = val[:, where].astype(F32)
            cons[pl.ds(line, 4, stride=LINES), :] = con_mine[:, where].astype(F32)
            cons[pl.ds(4 * LINES + line, 4, stride=LINES), :] = con_other[:, where].astype(F32)
        return carry

    lax.fori_loop(0, M1, spread, 0)

    is_first = band == 0
    first_count = jnp.where(is_first, mine[2 * SLOTS], other[2 * SLOTS])
    both_count = mine[2 * SLOTS] + other[2 * SLOTS]
    lane = lax.broadcasted_iota(jnp.int32, (1, LANES), 1) & 15
    gap = jnp.ones((1, LANES), F32)
    for p in range(HALF):
        pos = band * HALF + p
        from_first = pos < first_count
        slot = jnp.minimum(jnp.where(from_first, pos, pos - first_count), SLOTS - 1)
        own = from_first == is_first
        v = jnp.where(own, mine[slot], other[slot])
        c = jnp.where(own, mine[SLOTS + slot], other[SLOTS + slot])
        gap = jnp.where(lane == p, con_e[c] - val_e[v], gap)
        v_line = v * LINES
        c_line = (jnp.where(own, 0, 4) + (c & 3)) * LINES

        def product(t, carry):
            made = vals[pl.ds(v_line + t * M1, M1), :] * cons[pl.ds(c_line + t * M1, M1), :]
            high = made.astype(BF16)
            where = pl.ds(pl.multiple_of(t * LANES, LANES), LANES)
            lhs[p * M1 : (p + 1) * M1, where] = high
            lhs[HALF * M1 + p * M1 : HALF * M1 + (p + 1) * M1, where] = (
                made - high.astype(F32)
            ).astype(BF16)
            return carry

        lax.fori_loop(0, CHUNKS, product, 0, unroll=4)

    acc[...] = jnp.zeros_like(acc)

    def transform(k, carry):
        for i in range(STEP // M3):
            table[i * M3 : (i + 1) * M3, :] = (
                second[pl.ds(k * (STEP // M3) + i, 1), :] * third[...]
            ).astype(BF16)
        where = pl.ds(pl.multiple_of(k * STEP, STEP), STEP)
        acc[...] += jnp.dot(
            lhs[: HALF * M1, where], table[...], preferred_element_type=F32
        ) + jnp.dot(lhs[HALF * M1 :, where], table[...], preferred_element_type=F32)
        return carry

    lax.fori_loop(0, KP // STEP, transform, 0)
    mid = acc[...]
    mid_hi = mid.astype(BF16)
    mid_lo = (mid - mid_hi.astype(F32)).astype(BF16)
    done[...] = (
        jnp.dot(mix_hi[...], mid_hi, preferred_element_type=F32)
        + jnp.dot(mix_hi[...], mid_lo, preferred_element_type=F32)
        + jnp.dot(mix_lo[...], mid_hi, preferred_element_type=F32)
    )

    at_lane = lax.broadcasted_iota(jnp.int32, (1, LANES), 1)
    frequency = (at_lane >> 4).astype(F32)
    live = (band * HALF + lane < both_count) & (lane < HALF) & (at_lane < 32)
    weight = jnp.where(
        live, 2.0 * gap / (gap * gap + frequency * frequency), 0.0
    ) * (1.0 / math.sqrt(TOTAL))
    w_hi = weight.astype(BF16).astype(F32)
    w_mid = (weight - w_hi).astype(BF16).astype(F32)
    lines[WIDTH * HALF : WIDTH * HALF + 1, :] = w_hi
    lines[WIDTH * HALF + 1 : WIDTH * HALF + 2, :] = w_mid
    lines[WIDTH * HALF + 2 : WIDTH * HALF + 3, :] = weight - w_hi - w_mid
    lines[WIDTH * HALF + 3 : WIDTH * HALF + 4, :] = jnp.zeros((1, LANES), F32)

    norm = 1.0 / math.sqrt(MG)
    for k in range(N1):
        block = done[k * 16 : (k + 1) * 16, :] * (scale[k : k + 1, :] * norm)
        for ch in range(WIDTH):
            piece = block[:HALF, ch * LANES : (ch + 1) * LANES]
            lines[ch * HALF : (ch + 1) * HALF, :] = piece
            at = (k % 2 * WIDTH + ch) * HALF
            row_lines[at : at + HALF, :] = piece
        col_out[k] = lines[...].astype(BF16)
        if k % 2 == 1:
            row_out[k // 2] = row_lines[...].astype(BF16)


def density_call(place, mine, other, val_e, con_e, val, con_mine, con_other, scale, interpret=False):
    second, third, (mix_hi, mix_lo) = tables()
    smem = pl.BlockSpec(memory_space=SMEM)
    vmem = pl.BlockSpec(memory_space=VMEM)
    return pl.pallas_call(
        density_kernel,
        out_shape=[
            jax.ShapeDtypeStruct((N1, BLOCK, LANES), BF16),
            jax.ShapeDtypeStruct((GROW, ROWBLOCK, LANES), BF16),
        ],
        in_specs=[smem] * 5 + [vmem] * 8,
        out_specs=[vmem] * 2,
        scratch_shapes=[
            VMEM((16 * LINES, LANES), F32),
            VMEM((8 * LINES, LANES), F32),
            VMEM((2 * HALF * M1, KP), BF16),
            VMEM((HALF * M1, NP), F32),
            VMEM((STEP, NP), BF16),
            VMEM((N1 * 16, NP), F32),
            VMEM((BLOCK, LANES), F32),
            VMEM((ROWBLOCK, LANES), F32),
        ],
        compiler_params=pltpu.CompilerParams(vmem_limit_bytes=34 << 20),
        interpret=interpret,
        name="density",
    )(place, mine, other, val_e, con_e, val, con_mine, con_other, scale,
      jnp.asarray(second), jnp.asarray(third), jnp.asarray(mix_hi), jnp.asarray(mix_lo))


def pack_kernel(place, blocks, out, spread):
    z = (place[0] >> 4) & 7
    stride = ROWBLOCK + 4
    for i in range(GROW):
        spread[i * stride : i * stride + ROWBLOCK, :] = blocks[(z + ZAROUND[i]) & 7].astype(F32)
    for ch in range(2 * WIDTH):
        for pp in range(HALF // 2):
            got = [
                spread[pl.ds(ch * HALF + 2 * pp + q, GROW, stride=stride), :] for q in range(2)
            ]
            out[pp * 16 : (pp + 1) * 16, ch * LANES : (ch + 1) * LANES] = jnp.concatenate(
                got, 0
            ).astype(BF16)


def pack_call(place, blocks, interpret=False):
    vmem = pl.BlockSpec(memory_space=VMEM)
    return pl.pallas_call(
        pack_kernel,
        out_shape=jax.ShapeDtypeStruct((GROW * HALF, ROW), BF16),
        in_specs=[pl.BlockSpec(memory_space=SMEM), vmem],
        out_specs=vmem,
        scratch_shapes=[VMEM((GROW * (ROWBLOCK + 4), LANES), F32)],
        compiler_params=pltpu.CompilerParams(vmem_limit_bytes=4 << 20),
        interpret=interpret,
        name="pack",
    )(place, blocks)


def fetch(pieces, rows, sems):
    copies = []
    at = 0
    for i, piece in enumerate(pieces):
        size = piece.shape[0]
        copies.append(pltpu.make_async_copy(piece, rows.at[pl.ds(at, size), :], sems.at[i]))
        copies[-1].start()
        at += size
    return copies


def around(step):
    return jnp.where(step == 0, 0, jnp.where(step == 1, 3, jnp.where(step == 2, 1, 2)))


def assemble_kernel(place, *refs):
    cols = refs[:GROW]
    away_out, home_out, spread = refs[GROW:]
    me = place[0]
    band, y, x = me >> 7, (me >> 2) & 3, me & 3
    for i, col in enumerate(cols):
        for q in range(GCOL):
            at = i * COLROWS + q * BLOCK
            spread[at : at + BLOCK, :] = col[q].astype(F32)

    def assemble(j, carry):
        outer, inner = around(j >> 2), around(j & 3)
        dy = jnp.where(band == 0, outer, inner)
        dx = jnp.where(band == 0, inner, outer)
        base = (((y + dy) & 3) * 4 + ((x + dx) & 3)) * BLOCK
        weight = jnp.zeros((GROW, LANES), F32)
        for part in range(3):
            weight += spread[pl.ds(base + WIDTH * HALF + part, GROW, stride=COLROWS), :]
        other = pltpu.roll(weight, LANES - 16, 1)
        away = jnp.where(band == 0, other, weight)
        home = jnp.where(band == 0, weight, other)
        for pp in range(HALF // 2):
            ws = [
                [jnp.broadcast_to(w[:, 2 * pp + q : 2 * pp + q + 1], (GROW, LANES)) for q in range(2)]
                for w in (away, home)
            ]
            to = pl.ds(pl.multiple_of(j * GROW * HALF + pp * 16, 16), 16)
            for ch in range(WIDTH):
                got = [
                    spread[pl.ds(base + ch * HALF + 2 * pp + q, GROW, stride=COLROWS), :]
                    for q in range(2)
                ]
                where = slice(ch * LANES, (ch + 1) * LANES)
                for f, dest in enumerate((away_out, home_out)):
                    dest[to, where] = jnp.concatenate(
                        [got[0] * ws[f][0], got[1] * ws[f][1]], 0
                    ).astype(BF16)
        return carry

    lax.fori_loop(0, GCOL, assemble, 0)


def assemble_call(place, cols, interpret=False):
    vmem = pl.BlockSpec(memory_space=VMEM)
    return pl.pallas_call(
        assemble_kernel,
        out_shape=[jax.ShapeDtypeStruct((PANEL, NP), BF16)] * 2,
        in_specs=[pl.BlockSpec(memory_space=SMEM)] + [vmem] * GROW,
        out_specs=[vmem] * 2,
        scratch_shapes=[VMEM((GROW * COLROWS, LANES), F32)],
        compiler_params=pltpu.CompilerParams(vmem_limit_bytes=14 << 20),
        interpret=interpret,
        name="assemble",
    )(place, *cols)


def away_kernel(weighted, *refs):
    pieces = refs[:5]
    away_out, turned_out, rows, sems = refs[5:]
    for copy in fetch(pieces, rows, sems):
        copy.wait()

    def product(m, carry):
        where = pl.ds(pl.multiple_of(m * 256, 256), 256)
        part = rows[:, where].T
        turned_out[where, :] = part
        away_out[where, :] = jnp.dot(part, weighted[...], preferred_element_type=F32).astype(BF16)
        return carry

    lax.fori_loop(0, ROW // 256, product, 0)


def away_call(weighted, pieces, interpret=False):
    vmem = pl.BlockSpec(memory_space=VMEM)
    return pl.pallas_call(
        away_kernel,
        out_shape=(
            jax.ShapeDtypeStruct((ROW, NP), BF16),
            jax.ShapeDtypeStruct((ROW, PANEL), BF16),
        ),
        in_specs=[vmem] + [pl.BlockSpec(memory_space=pl.ANY)] * 5,
        out_specs=(vmem, vmem),
        scratch_shapes=[VMEM((PANEL, ROW), BF16), pltpu.SemaphoreType.DMA((5,))],
        compiler_params=pltpu.CompilerParams(vmem_limit_bytes=20 << 20),
        interpret=interpret,
        name="away",
    )(weighted, *pieces)


def home_kernel(weighted, rows, home_out):
    def product(m, carry):
        where = pl.ds(pl.multiple_of(m * 256, 256), 256)
        home_out[where, :] = jnp.dot(rows[where, :], weighted[...], preferred_element_type=F32)
        return carry

    lax.fori_loop(0, ROW // 256, product, 0)


def home_call(weighted, rows, interpret=False):
    vmem = pl.BlockSpec(memory_space=VMEM)
    return pl.pallas_call(
        home_kernel,
        out_shape=jax.ShapeDtypeStruct((ROW, NP), F32),
        in_specs=[vmem, vmem],
        out_specs=vmem,
        compiler_params=pltpu.CompilerParams(vmem_limit_bytes=16 << 20),
        interpret=interpret,
        name="home",
    )(weighted, rows)


PLANE = ("band", "gcol_0", "gcol_1")


def turned(array, phase, step):
    pairs = []
    for band in range(2):
        along_x = (band == 0) == (phase == 0)
        for y in range(4):
            for x in range(4):
                to = (y, (x + step) % 4) if along_x else ((y + step) % 4, x)
                pairs.append((band * 16 + y * 4 + x, band * 16 + to[0] * 4 + to[1]))
    return lax.ppermute(array, PLANE, pairs)


def up(array, step):
    return lax.ppermute(array, "grow", [(i, (i + step) % GROW) for i in range(GROW)])


def swap(array):
    return lax.ppermute(array, "band", [(0, 1), (1, 0)])


def per_device(
    valence_orbitals,
    conduction_orbitals,
    valence_energy,
    conduction_energy,
    coulomb_root,
    pair_bands,
    slot_counts,
):
    place = lax.axis_index(("band", "grow", "gcol_0", "gcol_1")).astype(jnp.int32).reshape(1)
    meta = jnp.concatenate([pair_bands.reshape(2 * SLOTS), slot_counts, jnp.zeros(7, jnp.int32)])
    other_con = swap(conduction_orbitals)
    other_meta = swap(meta)
    scale = coulomb_root.reshape(N1, NP)
    col, row = density_call(
        place, meta, other_meta, valence_energy, conduction_energy,
        valence_orbitals, conduction_orbitals, other_con, scale,
    )
    return exchange(place, col, row)


def exchange(place, col, row):
    row = lax.all_to_all(row, "grow", 0, 0, tiled=True)
    col = lax.all_to_all(col, ("gcol_0", "gcol_1"), 0, 0, tiled=True)
    row = pack_call(place, row)
    ups, downs = [col], [col]
    for _ in range(1, 5):
        ups.append(up(ups[-1], 1))
    for _ in range(1, 4):
        downs.append(up(downs[-1], -1))
    half = row.shape[0] // 2
    below, above = turned(row, 0, 1), turned(row, 0, -1)
    far_a, far_b = turned(below[:half], 0, 1), turned(above[half:], 0, -1)
    line = jnp.concatenate([row, below, above, far_a, far_b], 0)
    half = line.shape[0] // 2
    below, above = turned(line, 1, 1), turned(line, 1, -1)
    far_a, far_b = turned(below[:half], 1, 1), turned(above[half:], 1, -1)
    weighted_away, weighted_home = assemble_call(place, ups + downs[1:])
    away, turned_rows = away_call(weighted_away, [line, below, above, far_a, far_b])
    received = swap(away)
    home = home_call(weighted_home, turned_rows)
    return -(home + received.astype(F32))[None]


def solution(mesh):
    finer = Mesh(
        mesh.devices.reshape(mesh.shape["band"], mesh.shape["grow"], 4, 4),
        ("band", "grow", "gcol_0", "gcol_1"),
    )
    everywhere = ("band", "grow", "gcol_0", "gcol_1")
    in_specs = (P(), P(everywhere, None), P(), P(), P(), P(None, everywhere), P(everywhere))
    return jax.shard_map(
        per_device,
        mesh=finer,
        in_specs=in_specs,
        out_specs=P("band", "grow", ("gcol_0", "gcol_1")),
        check_vma=False,
    )
```

profile of v0, /device:TPU:1, one launch (start us, length us, event | category | flops | bytes accessed | tf_op | source)
XLA Modules:
  0.0 131.2 jit_solution(8202818933629378848)
XLA Ops:
  0.0 3.2 %collective-permute-start.1 = (bf16[4,98304]{1,0:T(4,128)(2,1)}, bf16[4,98304]{1,0:T(4,128)(2,1)S(1)}, u32[]{:S(2)}, u32[]{:S(2)}) collective-permute-start(bf16[4,98304]{1,0:T(4,128)(2,1)} %con_mine.1), channel_id=1, source_target_pairs={{0,128},{128,0},{1,129},{129,1},{2,130},{130,2},{3,131},{131,3},{4... | collective-permute-start | bytes 2359304 | tf_op jit(solution)/shard_map/ppermute | solution.py:361
  3.9 0.8 reshape.11
  4.6 0.1 pad_add_fusion.mine
  4.7 0.0 collective-permute-start
  4.7 0.8 reshape.12.scale
  5.6 0.3 collective-permute-done.other
  5.9 0.0 collective-permute-done.1.con_other
  5.9 0.0 copy-start
  5.9 1.9 %copy-done = bf16[16,98304]{1,0:T(8,128)(2,1)S(1)} copy-done((bf16[16,98304]{1,0:T(8,128)(2,1)S(1)}, bf16[16,98304]{1,0:T(8,128)(2,1)}, u32[]{:S(2)}) %copy-start) | copy-done | bytes 3145752
  7.8 0.0 copy-start.1
  7.8 1.1 copy-done.1
  8.9 0.0 copy-start.2
  8.9 0.9 copy-done.2
  9.8 0.0 copy-start.3
  9.8 0.9 copy-done.3
  10.8 0.0 copy-start.4
  10.8 0.9 copy-done.4
  11.7 0.0 copy-start.5
  11.7 0.9 copy-done.5
  12.6 0.0 copy-start.6
  12.6 0.7 copy-done.6
  13.3 0.0 copy-start.7
  13.3 0.7 copy-done.7
  13.9 8.9 %density.1 = (bf16[16,64,128]{2,1,0:T(8,128)(2,1)S(1)}, bf16[8,120,128]{2,1,0:T(8,128)(2,1)S(1)}) custom-call(s32[1]{0:T(128)} %bitcast.place, s32[48]{0:T(128)S(1)} %pad_add_fusion.mine, s32[48]{0:T(128)S(1)} %collective-permute-done.other, f32[16]{0:T(128)S(1)} %copy-done.7, f32[1024]{0:T(1024)S(1)} %copy-done.6, bf16[16,98304]{1,0:T(8,128)(2,1)S(1)} %copy-done, ...), custom_call_target="tpu_custom_call" | custom-call | tf_op jit(solution)/shard_map/density/pallas_call | solution.py:162
  22.8 17.7 %all_to_all.10.blocks = bf16[8,120,128]{2,1,0:T(8,128)(2,1)S(1)} all-to-all(bf16[8,120,128]{2,1,0:T(8,128)(2,1)S(1)} %get-tuple-element.14), channel_id=1, replica_groups=mesh['band'=2,'grow'=8,'gcol_0'=4,'gcol_1'=4] {'grow'}, dimensions={0} | all-to-all | bytes 491520 | tf_op jit(solution)/shard_map/all_to_all | solution.py:386
  40.6 0.1 pack.1
  40.6 2.8 %collective-permute-start.10 = (bf16[80,1536]{1,0:T(8,128)(2,1)S(1)}, bf16[80,1536]{1,0:T(8,128)(2,1)S(1)}, u32[]{:S(2)}, u32[]{:S(2)}) collective-permute-start(bf16[80,1536]{1,0:T(8,128)(2,1)S(1)} %pack.1), channel_id=1, source_target_pairs={{0,3},{1,0},{2,1},{3,2},{4,7},{5,4},{6,5},{7,6},{8,11},{9,8},{10,9... | collective-permute-start | bytes 737288 | tf_op jit(solution)/shard_map/ppermute | solution.py:353
  43.4 0.0 collective-permute-start.9
  43.4 3.1 %collective-permute-done.10 = bf16[80,1536]{1,0:T(8,128)(2,1)S(1)} collective-permute-done((bf16[80,1536]{1,0:T(8,128)(2,1)S(1)}, bf16[80,1536]{1,0:T(8,128)(2,1)S(1)}, u32[]{:S(2)}, u32[]{:S(2)}) %collective-permute-start.10) | collective-permute-done | bytes 245792 | tf_op jit(solution)/shard_map/ppermute | solution.py:353
  46.6 3.2 %collective-permute-start.12 = (bf16[40,1536]{1,0:T(8,128)(2,1)S(1)}, bf16[40,1536]{1,0:T(8,128)(2,1)S(1)}, u32[]{:S(2)}, u32[]{:S(2)}) collective-permute-start(bf16[40,1536]{1,0:T(8,128)(2,1)S(1)} %slice.17), channel_id=1, source_target_pairs={{0,3},{1,0},{2,1},{3,2},{4,7},{5,4},{6,5},{7,6},{8,11},{9,8},{10,9... | collective-permute-start | bytes 368648 | tf_op jit(solution)/shard_map/ppermute | solution.py:353
  49.8 0.2 collective-permute-done.9
  50.0 0.1 collective-permute-start.11
  50.1 4.9 %collective-permute-done.11 = bf16[40,1536]{1,0:T(8,128)(2,1)S(1)} collective-permute-done((bf16[40,1536]{1,0:T(8,128)(2,1)S(1)}, bf16[40,1536]{1,0:T(8,128)(2,1)S(1)}, u32[]{:S(2)}, u32[]{:S(2)}) %collective-permute-start.11) | collective-permute-done | bytes 122912 | tf_op jit(solution)/shard_map/ppermute | solution.py:353
  55.0 0.0 collective-permute-done.12
  55.0 3.0 %collective-permute-start.14 = (bf16[320,1536]{1,0:T(8,128)(2,1)S(1)}, bf16[320,1536]{1,0:T(8,128)(2,1)S(1)}, u32[]{:S(2)}, u32[]{:S(2)}) collective-permute-start(bf16[320,1536]{1,0:T(8,128)(2,1)S(1)} %constant_dynamic-update-slice_fusion.refs_0_), channel_id=1, source_target_pairs={{0,12},{1,13},{2,14},{3,15},{4,0},{5,1},{6,2},{7,3},{8,4},{9,5},{1... | collective-permute-start | bytes 2949128 | tf_op jit(solution)/shard_map/ppermute | solution.py:353
  58.1 0.0 collective-permute-start.13
  58.1 17.3 %all_to_all.11.refs_0_ = bf16[16,64,128]{2,1,0:T(8,128)(2,1)S(1)} all-to-all(bf16[16,64,128]{2,1,0:T(8,128)(2,1)S(1)} %get-tuple-element.11), channel_id=1, replica_groups=mesh['band'=2,'grow'=8,'gcol_0'=4,'gcol_1'=4] {'gcol_0','gcol_1'}, dimensions={0} | all-to-all | bytes 524288 | tf_op jit(solution)/shard_map/all_to_all | solution.py:387
  75.3 0.0 collective-permute-start.2
  75.3 2.7 %collective-permute-start.6 = (bf16[16,64,128]{2,1,0:T(8,128)(2,1)S(1)}, bf16[16,64,128]{2,1,0:T(8,128)(2,1)S(1)}, u32[]{:S(2)}, u32[]{:S(2)}) collective-permute-start(bf16[16,64,128]{2,1,0:T(8,128)(2,1)S(1)} %all_to_all.11.refs_0_), channel_id=1, source_target_pairs={{0,112},{16,0},{32,16},{48,32},{64,48},{80,64},{96,80},{112,96},{1... | collective-permute-start | bytes 786440 | tf_op jit(solution)/shard_map/ppermute | solution.py:357
  78.0 3.8 %collective-permute-done.2.refs_1_ = bf16[16,64,128]{2,1,0:T(8,128)(2,1)S(1)} collective-permute-done((bf16[16,64,128]{2,1,0:T(8,128)(2,1)S(1)}, bf16[16,64,128]{2,1,0:T(8,128)(2,1)S(1)}, u32[]{:S(2)}, u32[]{:S(2)}) %collective-permute-start.2) | collective-permute-done | bytes 262176 | tf_op jit(solution)/shard_map/ppermute | solution.py:357
  81.8 0.0 collective-permute-start.3
  81.8 0.0 collective-permute-done.6.refs_5_
  81.8 2.7 %collective-permute-start.7 = (bf16[16,64,128]{2,1,0:T(8,128)(2,1)S(1)}, bf16[16,64,128]{2,1,0:T(8,128)(2,1)S(1)}, u32[]{:S(2)}, u32[]{:S(2)}) collective-permute-start(bf16[16,64,128]{2,1,0:T(8,128)(2,1)S(1)} %collective-permute-done.6.refs_5_), channel_id=1, source_target_pairs={{0,112},{16,0},{32,16},{48,32},{64,48},{80,64},{96,80},{112,96},{1... | collective-permute-start | bytes 786440 | tf_op jit(solution)/shard_map/ppermute | solution.py:357
  84.5 4.7 %collective-permute-done.3.refs_2_ = bf16[16,64,128]{2,1,0:T(8,128)(2,1)S(1)} collective-permute-done((bf16[16,64,128]{2,1,0:T(8,128)(2,1)S(1)}, bf16[16,64,128]{2,1,0:T(8,128)(2,1)S(1)}, u32[]{:S(2)}, u32[]{:S(2)}) %collective-permute-start.3) | collective-permute-done | bytes 262176 | tf_op jit(solution)/shard_map/ppermute | solution.py:357
  89.1 0.0 collective-permute-start.4
  89.1 0.0 collective-permute-done.14.refs_2_
  89.2 0.3 collective-permute-start.16
  89.4 0.0 collective-permute-done.13.refs_1_
  89.5 1.5 %collective-permute-start.15 = (bf16[160,1536]{1,0:T(8,128)(2,1)S(1)}, bf16[160,1536]{1,0:T(8,128)(2,1)S(1)}, u32[]{:S(2)}, u32[]{:S(2)}) collective-permute-start(bf16[160,1536]{1,0:T(8,128)(2,1)S(1)} %slice.18), channel_id=1, source_target_pairs={{0,4},{1,5},{2,6},{3,7},{4,8},{5,9},{6,10},{7,11},{8,12},{9,13},{1... | collective-permute-start | bytes 1474568 | tf_op jit(solution)/shard_map/ppermute | solution.py:353
  91.0 0.0 collective-permute-done.7.refs_6_
  91.0 2.7 %collective-permute-start.8 = (bf16[16,64,128]{2,1,0:T(8,128)(2,1)S(1)}, bf16[16,64,128]{2,1,0:T(8,128)(2,1)S(1)}, u32[]{:S(2)}, u32[]{:S(2)}) collective-permute-start(bf16[16,64,128]{2,1,0:T(8,128)(2,1)S(1)} %collective-permute-done.7.refs_6_), channel_id=1, source_target_pairs={{0,112},{16,0},{32,16},{48,32},{64,48},{80,64},{96,80},{112,96},{1... | collective-permute-start | bytes 786440 | tf_op jit(solution)/shard_map/ppermute | solution.py:357
  93.7 3.9 %collective-permute-done.4.refs_3_ = bf16[16,64,128]{2,1,0:T(8,128)(2,1)S(1)} collective-permute-done((bf16[16,64,128]{2,1,0:T(8,128)(2,1)S(1)}, bf16[16,64,128]{2,1,0:T(8,128)(2,1)S(1)}, u32[]{:S(2)}, u32[]{:S(2)}) %collective-permute-start.4) | collective-permute-done | bytes 262176 | tf_op jit(solution)/shard_map/ppermute | solution.py:357
  97.6 0.0 collective-permute-start.5
  97.6 0.1 collective-permute-done.8.refs_7_
  97.7 9.0 %collective-permute-done.5.refs_4_ = bf16[16,64,128]{2,1,0:T(8,128)(2,1)S(1)} collective-permute-done((bf16[16,64,128]{2,1,0:T(8,128)(2,1)S(1)}, bf16[16,64,128]{2,1,0:T(8,128)(2,1)S(1)}, u32[]{:S(2)}, u32[]{:S(2)}) %collective-permute-start.5) | collective-permute-done | bytes 262176 | tf_op jit(solution)/shard_map/ppermute | solution.py:357
  106.8 3.2 %assemble.1 = (bf16[1280,768]{1,0:T(8,128)(2,1)S(1)}, bf16[1280,768]{1,0:T(8,128)(2,1)S(1)}) custom-call(s32[1]{0:T(128)} %bitcast.place, bf16[16,64,128]{2,1,0:T(8,128)(2,1)S(1)} %all_to_all.11.refs_0_, bf16[16,64,128]{2,1,0:T(8,128)(2,1)S(1)} %collective-permute-done.2.refs_1_, bf16[16,64,128]{2,1,0:T(8,128)(2,1)S(1)} %collective-permute-done.3.refs_2_, ...), custom_call_target="tpu_custom_call" | custom-call | tf_op jit(solution)/shard_map/assemble/pallas_call | solution.py:275
  110.0 0.0 collective-permute-done.16.refs_4_
  110.0 0.0 collective-permute-done.15.refs_3_
  110.0 5.9 %away.1 = (bf16[1536,768]{1,0:T(8,128)(2,1)S(1)}, bf16[1536,1280]{1,0:T(8,128)(2,1)S(1)}) custom-call(bf16[1280,768]{1,0:T(8,128)(2,1)S(1)} %get-tuple-element.13.weighted, bf16[320,1536]{1,0:T(8,128)(2,1)S(1)} %constant_dynamic-update-slice_fusion.refs_0_, bf16[320,1536]{1,0:T(8,128)(2,1)S(1)} %collective-permute-done.13.refs_1_, ...), custom_call_target="tpu_custom_call" | custom-call | tf_op jit(solution)/shard_map/away/pallas_call | solution.py:305
  115.9 8.4 %collective-permute-start.17 = (bf16[1536,768]{1,0:T(8,128)(2,1)S(1)}, bf16[1536,768]{1,0:T(8,128)(2,1)S(1)}, u32[]{:S(2)}, u32[]{:S(2)}) collective-permute-start(bf16[1536,768]{1,0:T(8,128)(2,1)S(1)} %get-tuple-element.16), channel_id=1, source_target_pairs={{0,128},{128,0},{1,129},{129,1},{2,130},{130,2},{3,131},{131,3},{4... | collective-permute-start | bytes 7077896 | tf_op jit(solution)/shard_map/ppermute | solution.py:361
  124.4 4.1 %home.1 = f32[1536,768]{1,0:T(8,128)S(1)} custom-call(bf16[1280,768]{1,0:T(8,128)(2,1)S(1)} %get-tuple-element.12.weighted, bf16[1536,1280]{1,0:T(8,128)(2,1)S(1)} %get-tuple-element.15.rows), custom_call_target="tpu_custom_call" | custom-call | tf_op jit(solution)/shard_map/home/pallas_call | solution.py:331
  128.5 0.1 collective-permute-done.17
  128.5 2.6 %negate_bitcast_fusion = f32[1,1536,768]{2,1,0:T(8,128)} fusion(f32[1536,768]{1,0:T(8,128)S(1)} %home.1, bf16[1536,768]{1,0:T(8,128)(2,1)S(1)} %collective-permute-done.17), kind=kLoop, calls=%fused_computation | loop fusion | flops 3538944 | bytes 11796480 | tf_op jit(solution)/shard_map/neg | solution.py:405
  (10 shorter events, 0.2 us)
Async XLA Ops:
  0.0 5.9 %collective-permute-start.1 = (bf16[4,98304]{1,0:T(4,128)(2,1)}, bf16[4,98304]{1,0:T(4,128)(2,1)S(1)}, u32[]{:S(2)}, u32[]{:S(2)}) collective-permute-start(bf16[4,98304]{1,0:T(4,128)(2,1)} %con_mine.1), channel_id=1, source_target_pairs={{0,128},{128,0},{1,129},{129,1},{2,130},{130,2},{3,131},{131,3},{4... | collective-permute-start | bytes 2359304 | tf_op jit(solution)/shard_map/ppermute | solution.py:361
  4.7 1.2 collective-permute-start
  5.9 1.9 %copy-start = (bf16[16,98304]{1,0:T(8,128)(2,1)S(1)}, bf16[16,98304]{1,0:T(8,128)(2,1)}, u32[]{:S(2)}) copy-start(bf16[16,98304]{1,0:T(8,128)(2,1)} %val.1) | copy-start | bytes 9437188
  7.8 1.1 copy-start.1
  8.9 0.9 copy-start.2
  9.8 0.9 copy-start.3
  10.8 0.9 copy-start.4
  11.7 0.9 copy-start.5
  12.6 0.7 copy-start.6
  13.3 0.7 copy-start.7
  40.6 5.9 %collective-permute-start.10 = (bf16[80,1536]{1,0:T(8,128)(2,1)S(1)}, bf16[80,1536]{1,0:T(8,128)(2,1)S(1)}, u32[]{:S(2)}, u32[]{:S(2)}) collective-permute-start(bf16[80,1536]{1,0:T(8,128)(2,1)S(1)} %pack.1), channel_id=1, source_target_pairs={{0,3},{1,0},{2,1},{3,2},{4,7},{5,4},{6,5},{7,6},{8,11},{9,8},{10,9... | collective-permute-start | bytes 737288 | tf_op jit(solution)/shard_map/ppermute | solution.py:353
  43.4 6.6 %collective-permute-start.9 = (bf16[80,1536]{1,0:T(8,128)(2,1)S(1)}, bf16[80,1536]{1,0:T(8,128)(2,1)S(1)}, u32[]{:S(2)}, u32[]{:S(2)}) collective-permute-start(bf16[80,1536]{1,0:T(8,128)(2,1)S(1)} %pack.1), channel_id=1, source_target_pairs={{0,1},{1,2},{2,3},{3,0},{4,5},{5,6},{6,7},{7,4},{8,9},{9,10},{10,1... | collective-permute-start | bytes 737288 | tf_op jit(solution)/shard_map/ppermute | solution.py:353
  46.6 8.4 %collective-permute-start.12 = (bf16[40,1536]{1,0:T(8,128)(2,1)S(1)}, bf16[40,1536]{1,0:T(8,128)(2,1)S(1)}, u32[]{:S(2)}, u32[]{:S(2)}) collective-permute-start(bf16[40,1536]{1,0:T(8,128)(2,1)S(1)} %slice.17), channel_id=1, source_target_pairs={{0,3},{1,0},{2,1},{3,2},{4,7},{5,4},{6,5},{7,6},{8,11},{9,8},{10,9... | collective-permute-start | bytes 368648 | tf_op jit(solution)/shard_map/ppermute | solution.py:353
  50.0 5.0 %collective-permute-start.11 = (bf16[40,1536]{1,0:T(8,128)(2,1)S(1)}, bf16[40,1536]{1,0:T(8,128)(2,1)S(1)}, u32[]{:S(2)}, u32[]{:S(2)}) collective-permute-start(bf16[40,1536]{1,0:T(8,128)(2,1)S(1)} %slice.16), channel_id=1, source_target_pairs={{0,1},{1,2},{2,3},{3,0},{4,5},{5,6},{6,7},{7,4},{8,9},{9,10},{10,1... | collective-permute-start | bytes 368648 | tf_op jit(solution)/shard_map/ppermute | solution.py:353
  55.0 34.1 %collective-permute-start.14 = (bf16[320,1536]{1,0:T(8,128)(2,1)S(1)}, bf16[320,1536]{1,0:T(8,128)(2,1)S(1)}, u32[]{:S(2)}, u32[]{:S(2)}) collective-permute-start(bf16[320,1536]{1,0:T(8,128)(2,1)S(1)} %constant_dynamic-update-slice_fusion.refs_0_), channel_id=1, source_target_pairs={{0,12},{1,13},{2,14},{3,15},{4,0},{5,1},{6,2},{7,3},{8,4},{9,5},{1... | collective-permute-start | bytes 2949128 | tf_op jit(solution)/shard_map/ppermute | solution.py:353
  58.1 31.4 %collective-permute-start.13 = (bf16[320,1536]{1,0:T(8,128)(2,1)S(1)}, bf16[320,1536]{1,0:T(8,128)(2,1)S(1)}, u32[]{:S(2)}, u32[]{:S(2)}) collective-permute-start(bf16[320,1536]{1,0:T(8,128)(2,1)S(1)} %constant_dynamic-update-slice_fusion.refs_0_), channel_id=1, source_target_pairs={{0,4},{1,5},{2,6},{3,7},{4,8},{5,9},{6,10},{7,11},{8,12},{9,13},{1... | collective-permute-start | bytes 2949128 | tf_op jit(solution)/shard_map/ppermute | solution.py:353
  75.3 6.4 %collective-permute-start.2 = (bf16[16,64,128]{2,1,0:T(8,128)(2,1)S(1)}, bf16[16,64,128]{2,1,0:T(8,128)(2,1)S(1)}, u32[]{:S(2)}, u32[]{:S(2)}) collective-permute-start(bf16[16,64,128]{2,1,0:T(8,128)(2,1)S(1)} %all_to_all.11.refs_0_), channel_id=1, source_target_pairs={{0,16},{16,32},{32,48},{48,64},{64,80},{80,96},{96,112},{112,0},{1... | collective-permute-start | bytes 786440 | tf_op jit(solution)/shard_map/ppermute | solution.py:357
  75.3 6.4 %collective-permute-start.6 = (bf16[16,64,128]{2,1,0:T(8,128)(2,1)S(1)}, bf16[16,64,128]{2,1,0:T(8,128)(2,1)S(1)}, u32[]{:S(2)}, u32[]{:S(2)}) collective-permute-start(bf16[16,64,128]{2,1,0:T(8,128)(2,1)S(1)} %all_to_all.11.refs_0_), channel_id=1, source_target_pairs={{0,112},{16,0},{32,16},{48,32},{64,48},{80,64},{96,80},{112,96},{1... | collective-permute-start | bytes 786440 | tf_op jit(solution)/shard_map/ppermute | solution.py:357
  81.8 7.4 %collective-permute-start.3 = (bf16[16,64,128]{2,1,0:T(8,128)(2,1)S(1)}, bf16[16,64,128]{2,1,0:T(8,128)(2,1)S(1)}, u32[]{:S(2)}, u32[]{:S(2)}) collective-permute-start(bf16[16,64,128]{2,1,0:T(8,128)(2,1)S(1)} %collective-permute-done.2.refs_1_), channel_id=1, source_target_pairs={{0,16},{16,32},{32,48},{48,64},{64,80},{80,96},{96,112},{112,0},{1... | collective-permute-start | bytes 786440 | tf_op jit(solution)/shard_map/ppermute | solution.py:357
  81.8 9.2 %collective-permute-start.7 = (bf16[16,64,128]{2,1,0:T(8,128)(2,1)S(1)}, bf16[16,64,128]{2,1,0:T(8,128)(2,1)S(1)}, u32[]{:S(2)}, u32[]{:S(2)}) collective-permute-start(bf16[16,64,128]{2,1,0:T(8,128)(2,1)S(1)} %collective-permute-done.6.refs_5_), channel_id=1, source_target_pairs={{0,112},{16,0},{32,16},{48,32},{64,48},{80,64},{96,80},{112,96},{1... | collective-permute-start | bytes 786440 | tf_op jit(solution)/shard_map/ppermute | solution.py:357
  89.1 8.5 %collective-permute-start.4 = (bf16[16,64,128]{2,1,0:T(8,128)(2,1)S(1)}, bf16[16,64,128]{2,1,0:T(8,128)(2,1)S(1)}, u32[]{:S(2)}, u32[]{:S(2)}) collective-permute-start(bf16[16,64,128]{2,1,0:T(8,128)(2,1)S(1)} %collective-permute-done.3.refs_2_), channel_id=1, source_target_pairs={{0,16},{16,32},{32,48},{48,64},{64,80},{80,96},{96,112},{112,0},{1... | collective-permute-start | bytes 786440 | tf_op jit(solution)/shard_map/ppermute | solution.py:357
  89.2 20.8 %collective-permute-start.16 = (bf16[160,1536]{1,0:T(8,128)(2,1)S(1)}, bf16[160,1536]{1,0:T(8,128)(2,1)S(1)}, u32[]{:S(2)}, u32[]{:S(2)}) collective-permute-start(bf16[160,1536]{1,0:T(8,128)(2,1)S(1)} %slice.19), channel_id=1, source_target_pairs={{0,12},{1,13},{2,14},{3,15},{4,0},{5,1},{6,2},{7,3},{8,4},{9,5},{1... | collective-permute-start | bytes 1474568 | tf_op jit(solution)/shard_map/ppermute | solution.py:353
  89.5 20.5 %collective-permute-start.15 = (bf16[160,1536]{1,0:T(8,128)(2,1)S(1)}, bf16[160,1536]{1,0:T(8,128)(2,1)S(1)}, u32[]{:S(2)}, u32[]{:S(2)}) collective-permute-start(bf16[160,1536]{1,0:T(8,128)(2,1)S(1)} %slice.18), channel_id=1, source_target_pairs={{0,4},{1,5},{2,6},{3,7},{4,8},{5,9},{6,10},{7,11},{8,12},{9,13},{1... | collective-permute-start | bytes 1474568 | tf_op jit(solution)/shard_map/ppermute | solution.py:353
  91.0 6.7 %collective-permute-start.8 = (bf16[16,64,128]{2,1,0:T(8,128)(2,1)S(1)}, bf16[16,64,128]{2,1,0:T(8,128)(2,1)S(1)}, u32[]{:S(2)}, u32[]{:S(2)}) collective-permute-start(bf16[16,64,128]{2,1,0:T(8,128)(2,1)S(1)} %collective-permute-done.7.refs_6_), channel_id=1, source_target_pairs={{0,112},{16,0},{32,16},{48,32},{64,48},{80,64},{96,80},{112,96},{1... | collective-permute-start | bytes 786440 | tf_op jit(solution)/shard_map/ppermute | solution.py:357
  97.6 9.1 %collective-permute-start.5 = (bf16[16,64,128]{2,1,0:T(8,128)(2,1)S(1)}, bf16[16,64,128]{2,1,0:T(8,128)(2,1)S(1)}, u32[]{:S(2)}, u32[]{:S(2)}) collective-permute-start(bf16[16,64,128]{2,1,0:T(8,128)(2,1)S(1)} %collective-permute-done.4.refs_3_), channel_id=1, source_target_pairs={{0,16},{16,32},{32,48},{48,64},{64,80},{80,96},{96,112},{112,0},{1... | collective-permute-start | bytes 786440 | tf_op jit(solution)/shard_map/ppermute | solution.py:357
  115.9 12.6 %collective-permute-start.17 = (bf16[1536,768]{1,0:T(8,128)(2,1)S(1)}, bf16[1536,768]{1,0:T(8,128)(2,1)S(1)}, u32[]{:S(2)}, u32[]{:S(2)}) collective-permute-start(bf16[1536,768]{1,0:T(8,128)(2,1)S(1)} %get-tuple-element.16), channel_id=1, source_target_pairs={{0,128},{128,0},{1,129},{129,1},{2,130},{130,2},{3,131},{131,3},{4... | collective-permute-start | bytes 7077896 | tf_op jit(solution)/shard_map/ppermute | solution.py:361
where the time goes:
time: 132 us; the launch traced here: 131 us
  blocking collectives  35 us (27%)
  starting transfers between devices  30.6 us (23%)
  waiting for transfers between devices  30.1 us (23%)
  Pallas kernels  22.2 us (17%)
  local copies, waits for them, and re-layouts  9.78 us (7%)
  other arithmetic  2.72 us (2%)
    ppermute x7, waiting for transfers between devices, up(): lax.ppermute(array, 'grow', [(i, (i + step) % GROW) for i in range(GROW)])  21.5 us
    all_to_all x1, blocking collectives, exchange(): row = lax.all_to_all(row, 'grow', 0, 0, tiled=True)  17.7 us
    all_to_all x1, blocking collectives, exchange(): col = lax.all_to_all(col, ('gcol_0', 'gcol_1'), 0, 0, tiled=True)  17.3 us
    ppermute x3, starting transfers between devices, swap(): return lax.ppermute(array, 'band', [(0, 1), (1, 0)])  11.6 us
    ppermute x8, starting transfers between devices, turned(): return lax.ppermute(array, PLANE, pairs)  10.9 us
    pallas_call x1, Pallas kernels, density_call(): pl.pallas_call(density_kernel, out_shape=[jax.ShapeDtypeStruct((N1, BLOCK...  8.89 us
    ppermute x8, waiting for transfers between devices, turned(): return lax.ppermute(array, PLANE, pairs)  8.21 us
    unnamed x20, local copies, waits for them, and re-layouts  8.12 us
  transfers between devices with their start and end apart: 18, of which 10 were waited for; matrix products, arithmetic and copies ran while one was open for 1% of the time, Pallas kernels for 6%

commit v1 on v0

--- a/solution.py
+++ b/solution.py
@@ -61,22 +61,32 @@
 
 
 def density_kernel(
-    place, mine, other, val_e, con_e, val, con_mine, con_other, scale, second, third, mix_hi, mix_lo,
-    *refs,
+    place, mine, other, *refs,
 ):
-    col_out, row_out, vals, cons, lhs, acc, table, done, lines, row_lines = refs
+    hbm, refs = refs[:10], refs[10:]
+    col_out, row_out, vals, cons, lhs, acc, table_a, table_b, done, lines, row_lines = refs[:11]
+    local, sems = refs[11:21], refs[21]
+    copies = [pltpu.make_async_copy(a, b, sems.at[i]) for i, (a, b) in enumerate(zip(hbm, local))]
+    for copy in copies:
+        copy.start()
+    val, con_mine, con_other, second, third, mix_hi, mix_lo, scale, val_e, con_e = local
     band = place[0] >> 7
+    for copy in copies[:3]:
+        copy.wait()
 
     def spread(a, carry):
         for t in range(CHUNKS):
             where = pl.ds(pl.multiple_of(a * KP + t * LANES, LANES), LANES)
             line = t * M1 + a
             vals[pl.ds(line, 16, stride=LINES), :] = val[:, where].astype(F32)
-            cons[pl.ds(line, 4, stride=LINES), :] = con_mine[:, where].astype(F32)
-            cons[pl.ds(4 * LINES + line, 4, stride=LINES), :] = con_other[:, where].astype(F32)
+            cons[pl.ds(line, 8, stride=LINES), :] = jnp.concatenate(
+                [con_mine[:, where].astype(F32), con_other[:, where].astype(F32)], 0
+            )
         return carry
 
     lax.fori_loop(0, M1, spread, 0)
+    for copy in copies[3:]:
+        copy.wait()
 
     is_first = band == 0
     first_count = jnp.where(is_first, mine[2 * SLOTS], other[2 * SLOTS])
@@ -108,18 +118,29 @@
 
     acc[...] = jnp.zeros_like(acc)
 
-    def transform(k, carry):
+    def make(table, k):
         for i in range(STEP // M3):
             table[i * M3 : (i + 1) * M3, :] = (
                 second[pl.ds(k * (STEP // M3) + i, 1), :] * third[...]
             ).astype(BF16)
+
+    def add(table, k):
         where = pl.ds(pl.multiple_of(k * STEP, STEP), STEP)
         acc[...] += jnp.dot(
             lhs[: HALF * M1, where], table[...], preferred_element_type=F32
         ) + jnp.dot(lhs[HALF * M1 :, where], table[...], preferred_element_type=F32)
+
+    last = KP // STEP - 1
+    make(table_a, 0)
+
+    def transform(k, carry):
+        make(table_b, 2 * k + 1)
+        add(table_a, 2 * k)
+        make(table_a, jnp.minimum(2 * k + 2, last))
+        add(table_b, 2 * k + 1)
         return carry
 
-    lax.fori_loop(0, KP // STEP, transform, 0)
+    lax.fori_loop(0, KP // STEP // 2, transform, 0)
     mid = acc[...]
     mid_hi = mid.astype(BF16)
     mid_lo = (mid - mid_hi.astype(F32)).astype(BF16)
@@ -155,17 +176,23 @@
             row_out[k // 2] = row_lines[...].astype(BF16)
 
 
+def stay(array):
+    return pltpu.with_memory_space_constraint(jnp.asarray(array), pltpu.HBM)
+
+
 def density_call(place, mine, other, val_e, con_e, val, con_mine, con_other, scale, interpret=False):
     second, third, (mix_hi, mix_lo) = tables()
     smem = pl.BlockSpec(memory_space=SMEM)
     vmem = pl.BlockSpec(memory_space=VMEM)
+    hbm = pl.BlockSpec(memory_space=pltpu.HBM)
+    anywhere = pl.BlockSpec(memory_space=pl.ANY)
     return pl.pallas_call(
         density_kernel,
         out_shape=[
             jax.ShapeDtypeStruct((N1, BLOCK, LANES), BF16),
             jax.ShapeDtypeStruct((GROW, ROWBLOCK, LANES), BF16),
         ],
-        in_specs=[smem] * 5 + [vmem] * 8,
+        in_specs=[smem] * 3 + [hbm, hbm, anywhere] + [hbm] * 4 + [anywhere, hbm, hbm],
         out_specs=[vmem] * 2,
         scratch_shapes=[
             VMEM((16 * LINES, LANES), F32),
@@ -173,15 +200,27 @@
             VMEM((2 * HALF * M1, KP), BF16),
             VMEM((HALF * M1, NP), F32),
             VMEM((STEP, NP), BF16),
+            VMEM((STEP, NP), BF16),
             VMEM((N1 * 16, NP), F32),
             VMEM((BLOCK, LANES), F32),
             VMEM((ROWBLOCK, LANES), F32),
+            VMEM((16, MG), BF16),
+            VMEM((4, MG), BF16),
+            VMEM((4, MG), BF16),
+            VMEM((M2, NP), F32),
+            VMEM((M3, NP), F32),
+            VMEM((N1 * 16, HALF * M1), BF16),
+            VMEM((N1 * 16, HALF * M1), BF16),
+            VMEM((N1, NP), F32),
+            SMEM((16,), F32),
+            SMEM((1024,), F32),
+            pltpu.SemaphoreType.DMA((10,)),
         ],
         compiler_params=pltpu.CompilerParams(vmem_limit_bytes=34 << 20),
         interpret=interpret,
         name="density",
-    )(place, mine, other, val_e, con_e, val, con_mine, con_other, scale,
-      jnp.asarray(second), jnp.asarray(third), jnp.asarray(mix_hi), jnp.asarray(mix_lo))
+    )(place, mine, other, stay(val), stay(con_mine), con_other, stay(second), stay(third),
+      stay(mix_hi), stay(mix_lo), scale, stay(val_e), stay(con_e))
 
 
 def pack_kernel(place, blocks, out, spread):
@@ -391,10 +430,8 @@
         ups.append(up(ups[-1], 1))
     for _ in range(1, 4):
         downs.append(up(downs[-1], -1))
-    half = row.shape[0] // 2
-    below, above = turned(row, 0, 1), turned(row, 0, -1)
-    far_a, far_b = turned(below[:half], 0, 1), turned(above[half:], 0, -1)
-    line = jnp.concatenate([row, below, above, far_a, far_b], 0)
+    below, above, far = turned(row, 0, 1), turned(row, 0, -1), turned(row, 0, 2)
+    line = jnp.concatenate([row, below, above, far], 0)
     half = line.shape[0] // 2
     below, above = turned(line, 1, 1), turned(line, 1, -1)
     far_a, far_b = turned(below[:half], 1, 1), turned(above[half:], 1, -1)

time: 132 us -> 119 us (0.902); the launches traced: 131 us -> 117 us
  local copies, waits for them, and re-layouts: 9.78 us -> 1.64 us
  waiting for transfers between devices: 30.1 us -> 24.5 us
  starting transfers between devices: 30.6 us -> 27 us
  Pallas kernels: 22.2 us -> 23.9 us
    unnamed x20 -> x0, local copies, waits for them, and re-layouts: 8.12 us -> none
    ppermute x7, waiting for transfers between devices: 21.5 us -> 18.2 us  [up(): lax.ppermute(array, 'grow', [(i, (i + step) % GROW) for i in range(GROW)])]
    ppermute x8 -> x7, waiting for transfers between devices: 8.21 us -> 5.87 us  [turned(): return lax.ppermute(array, PLANE, pairs)]
    ppermute x8 -> x7, starting transfers between devices: 10.9 us -> 8.82 us  [turned(): return lax.ppermute(array, PLANE, pairs)]
    pallas_call x1, Pallas kernels: 8.89 us -> 10.6 us  [density_call(): pl.pallas_call(density_kernel, out_shape=[jax.ShapeDtypeStruct((N1, BLOCK...]
    ppermute x3, starting transfers between devices: 11.6 us -> 10.1 us  [swap(): return lax.ppermute(array, 'band', [(0, 1), (1, 0)])]
  transfers between devices with their start and end apart: 18 -> 17, of which waited for: 10 -> 10; matrix products, arithmetic and copies ran while one was open for 1% -> 1% of each run, Pallas kernels for 6% -> 6%
where the time goes in v1:
time: 119 us; the launch traced here: 117 us
  blocking collectives  36.3 us (31%)
  starting transfers between devices  27 us (23%)
  waiting for transfers between devices  24.5 us (21%)
  Pallas kernels  23.9 us (20%)
  other arithmetic  2.79 us (2%)
  local copies, waits for them, and re-layouts  1.64 us (1%)
    all_to_all x1, blocking collectives, exchange(): col = lax.all_to_all(col, ('gcol_0', 'gcol_1'), 0, 0, tiled=True)  18.5 us
    ppermute x7, waiting for transfers between devices, up(): lax.ppermute(array, 'grow', [(i, (i + step) % GROW) for i in range(GROW)])  18.2 us
    all_to_all x1, blocking collectives, exchange(): row = lax.all_to_all(row, 'grow', 0, 0, tiled=True)  17.8 us
    pallas_call x1, Pallas kernels, density_call(): pl.pallas_call(density_kernel, out_shape=[jax.ShapeDtypeStruct((N1, BLOCK...  10.6 us
    ppermute x3, starting transfers between devices, swap(): return lax.ppermute(array, 'band', [(0, 1), (1, 0)])  10.1 us
    ppermute x7, starting transfers between devices, turned(): return lax.ppermute(array, PLANE, pairs)  8.82 us
    ppermute x7, starting transfers between devices, up(): lax.ppermute(array, 'grow', [(i, (i + step) % GROW) for i in range(GROW)])  8.03 us
    pallas_call x1, Pallas kernels, away_call(): pl.pallas_call(away_kernel, out_shape=(jax.ShapeDtypeStruct((ROW, NP), BF...  5.94 us
  transfers between devices with their start and end apart: 17, of which 10 were waited for; matrix products, arithmetic and copies ran while one was open for 1% of the time, Pallas kernels for 6%

profile of v1, /device:TPU:1, one launch (start us, length us, event | category | flops | bytes accessed | tf_op | source)
XLA Modules:
  0.0 116.8 jit_solution(11923309105943831396)
XLA Ops:
  0.0 3.2 %collective-permute-start.1 = (bf16[4,98304]{1,0:T(4,128)(2,1)}, bf16[4,98304]{1,0:T(4,128)(2,1)S(1)}, u32[]{:S(2)}, u32[]{:S(2)}) collective-permute-start(bf16[4,98304]{1,0:T(4,128)(2,1)} %refs_1_.1), channel_id=1, source_target_pairs={{0,128},{128,0},{1,129},{129,1},{2,130},{130,2},{3,131},{131,3},{4... | collective-permute-start | bytes 2359304 | tf_op jit(solution)/shard_map/ppermute | solution.py:400
  3.9 0.8 reshape.11
  4.6 0.1 pad_add_fusion.mine
  4.7 0.0 collective-permute-start
  4.7 0.8 reshape.12.refs_7_
  5.6 0.3 collective-permute-done.other
  5.9 0.0 collective-permute-done.1.refs_2_
  5.9 10.6 %density.1 = (bf16[16,64,128]{2,1,0:T(8,128)(2,1)S(1)}, bf16[8,120,128]{2,1,0:T(8,128)(2,1)S(1)}) custom-call(s32[1]{0:T(128)} %bitcast.place, s32[48]{0:T(128)S(1)} %pad_add_fusion.mine, s32[48]{0:T(128)S(1)} %collective-permute-done.other, bf16[16,98304]{1,0:T(8,128)(2,1)} %refs_0_.1, bf16[4,98304]{1,0:T(4,128)(2,1)} %refs_1_.1, ...), custom_call_target="tpu_custom_call" | custom-call | tf_op jit(solution)/shard_map/density/pallas_call | solution.py:189
  16.5 17.8 %all_to_all.10.blocks = bf16[8,120,128]{2,1,0:T(8,128)(2,1)S(1)} all-to-all(bf16[8,120,128]{2,1,0:T(8,128)(2,1)S(1)} %get-tuple-element.14), channel_id=1, replica_groups=mesh['band'=2,'grow'=8,'gcol_0'=4,'gcol_1'=4] {'grow'}, dimensions={0} | all-to-all | bytes 491520 | tf_op jit(solution)/shard_map/all_to_all | solution.py:425
  34.3 0.1 pack.1
  34.3 3.0 %collective-permute-start.11 = (bf16[80,1536]{1,0:T(8,128)(2,1)S(1)}, bf16[80,1536]{1,0:T(8,128)(2,1)S(1)}, u32[]{:S(2)}, u32[]{:S(2)}) collective-permute-start(bf16[80,1536]{1,0:T(8,128)(2,1)S(1)} %pack.1), channel_id=1, source_target_pairs={{0,2},{1,3},{2,0},{3,1},{4,6},{5,7},{6,4},{7,5},{8,10},{9,11},{10,... | collective-permute-start | bytes 737288 | tf_op jit(solution)/shard_map/ppermute | solution.py:392
  37.3 0.8 collective-permute-start.10
  38.1 0.7 collective-permute-start.9
  38.8 2.5 %collective-permute-done.11 = bf16[80,1536]{1,0:T(8,128)(2,1)S(1)} collective-permute-done((bf16[80,1536]{1,0:T(8,128)(2,1)S(1)}, bf16[80,1536]{1,0:T(8,128)(2,1)S(1)}, u32[]{:S(2)}, u32[]{:S(2)}) %collective-permute-start.11) | collective-permute-done | bytes 245792 | tf_op jit(solution)/shard_map/ppermute | solution.py:392
  41.3 3.0 %collective-permute-done.10 = bf16[80,1536]{1,0:T(8,128)(2,1)S(1)} collective-permute-done((bf16[80,1536]{1,0:T(8,128)(2,1)S(1)}, bf16[80,1536]{1,0:T(8,128)(2,1)S(1)}, u32[]{:S(2)}, u32[]{:S(2)}) %collective-permute-start.10) | collective-permute-done | bytes 245792 | tf_op jit(solution)/shard_map/ppermute | solution.py:392
  44.3 0.4 collective-permute-done.9
  44.7 0.1 pad_maximum_fusion.refs_0_
  44.7 2.5 %collective-permute-start.13 = (bf16[320,1536]{1,0:T(8,128)(2,1)S(1)}, bf16[320,1536]{1,0:T(8,128)(2,1)S(1)}, u32[]{:S(2)}, u32[]{:S(2)}) collective-permute-start(bf16[320,1536]{1,0:T(8,128)(2,1)S(1)} %pad_maximum_fusion.refs_0_), channel_id=1, source_target_pairs={{0,12},{1,13},{2,14},{3,15},{4,0},{5,1},{6,2},{7,3},{8,4},{9,5},{1... | collective-permute-start | bytes 2949128 | tf_op jit(solution)/shard_map/ppermute | solution.py:392
  47.3 0.0 collective-permute-start.12
  47.3 18.5 %all_to_all.11.refs_0_ = bf16[16,64,128]{2,1,0:T(8,128)(2,1)S(1)} all-to-all(bf16[16,64,128]{2,1,0:T(8,128)(2,1)S(1)} %get-tuple-element.11), channel_id=1, replica_groups=mesh['band'=2,'grow'=8,'gcol_0'=4,'gcol_1'=4] {'gcol_0','gcol_1'}, dimensions={0} | all-to-all | bytes 524288 | tf_op jit(solution)/shard_map/all_to_all | solution.py:426
  65.8 0.0 collective-permute-start.2
  65.8 2.7 %collective-permute-start.6 = (bf16[16,64,128]{2,1,0:T(8,128)(2,1)S(1)}, bf16[16,64,128]{2,1,0:T(8,128)(2,1)S(1)}, u32[]{:S(2)}, u32[]{:S(2)}) collective-permute-start(bf16[16,64,128]{2,1,0:T(8,128)(2,1)S(1)} %all_to_all.11.refs_0_), channel_id=1, source_target_pairs={{0,112},{16,0},{32,16},{48,32},{64,48},{80,64},{96,80},{112,96},{1... | collective-permute-start | bytes 786440 | tf_op jit(solution)/shard_map/ppermute | solution.py:396
  68.5 3.8 %collective-permute-done.2.refs_1_ = bf16[16,64,128]{2,1,0:T(8,128)(2,1)S(1)} collective-permute-done((bf16[16,64,128]{2,1,0:T(8,128)(2,1)S(1)}, bf16[16,64,128]{2,1,0:T(8,128)(2,1)S(1)}, u32[]{:S(2)}, u32[]{:S(2)}) %collective-permute-start.2) | collective-permute-done | bytes 262176 | tf_op jit(solution)/shard_map/ppermute | solution.py:396
  72.2 0.0 collective-permute-start.3
  72.2 0.0 collective-permute-done.6.refs_5_
  72.2 2.7 %collective-permute-start.7 = (bf16[16,64,128]{2,1,0:T(8,128)(2,1)S(1)}, bf16[16,64,128]{2,1,0:T(8,128)(2,1)S(1)}, u32[]{:S(2)}, u32[]{:S(2)}) collective-permute-start(bf16[16,64,128]{2,1,0:T(8,128)(2,1)S(1)} %collective-permute-done.6.refs_5_), channel_id=1, source_target_pairs={{0,112},{16,0},{32,16},{48,32},{64,48},{80,64},{96,80},{112,96},{1... | collective-permute-start | bytes 786440 | tf_op jit(solution)/shard_map/ppermute | solution.py:396
  74.9 3.8 %collective-permute-done.3.refs_2_ = bf16[16,64,128]{2,1,0:T(8,128)(2,1)S(1)} collective-permute-done((bf16[16,64,128]{2,1,0:T(8,128)(2,1)S(1)}, bf16[16,64,128]{2,1,0:T(8,128)(2,1)S(1)}, u32[]{:S(2)}, u32[]{:S(2)}) %collective-permute-start.3) | collective-permute-done | bytes 262176 | tf_op jit(solution)/shard_map/ppermute | solution.py:396
  78.7 0.0 collective-permute-start.4
  78.7 0.0 collective-permute-done.13.refs_2_
  78.7 0.8 collective-permute-start.15
  79.5 0.0 collective-permute-done.12.refs_1_
  79.6 1.0 collective-permute-start.14
  80.5 0.0 collective-permute-done.7.refs_6_
  80.5 2.7 %collective-permute-start.8 = (bf16[16,64,128]{2,1,0:T(8,128)(2,1)S(1)}, bf16[16,64,128]{2,1,0:T(8,128)(2,1)S(1)}, u32[]{:S(2)}, u32[]{:S(2)}) collective-permute-start(bf16[16,64,128]{2,1,0:T(8,128)(2,1)S(1)} %collective-permute-done.7.refs_6_), channel_id=1, source_target_pairs={{0,112},{16,0},{32,16},{48,32},{64,48},{80,64},{96,80},{112,96},{1... | collective-permute-start | bytes 786440 | tf_op jit(solution)/shard_map/ppermute | solution.py:396
  83.2 2.4 %collective-permute-done.4.refs_3_ = bf16[16,64,128]{2,1,0:T(8,128)(2,1)S(1)} collective-permute-done((bf16[16,64,128]{2,1,0:T(8,128)(2,1)S(1)}, bf16[16,64,128]{2,1,0:T(8,128)(2,1)S(1)}, u32[]{:S(2)}, u32[]{:S(2)}) %collective-permute-start.4) | collective-permute-done | bytes 262176 | tf_op jit(solution)/shard_map/ppermute | solution.py:396
  85.6 0.0 collective-permute-start.5
  85.6 1.0 collective-permute-done.8.refs_7_
  86.5 7.4 %collective-permute-done.5.refs_4_ = bf16[16,64,128]{2,1,0:T(8,128)(2,1)S(1)} collective-permute-done((bf16[16,64,128]{2,1,0:T(8,128)(2,1)S(1)}, bf16[16,64,128]{2,1,0:T(8,128)(2,1)S(1)}, u32[]{:S(2)}, u32[]{:S(2)}) %collective-permute-start.5) | collective-permute-done | bytes 262176 | tf_op jit(solution)/shard_map/ppermute | solution.py:396
  93.9 3.2 %assemble.1 = (bf16[1280,768]{1,0:T(8,128)(2,1)S(1)}, bf16[1280,768]{1,0:T(8,128)(2,1)S(1)}) custom-call(s32[1]{0:T(128)} %bitcast.place, bf16[16,64,128]{2,1,0:T(8,128)(2,1)S(1)} %all_to_all.11.refs_0_, bf16[16,64,128]{2,1,0:T(8,128)(2,1)S(1)} %collective-permute-done.2.refs_1_, bf16[16,64,128]{2,1,0:T(8,128)(2,1)S(1)} %collective-permute-done.3.refs_2_, ...), custom_call_target="tpu_custom_call" | custom-call | tf_op jit(solution)/shard_map/assemble/pallas_call | solution.py:314
  97.2 0.0 collective-permute-done.15.refs_4_
  97.2 0.0 collective-permute-done.14.refs_3_
  97.2 5.9 %away.1 = (bf16[1536,768]{1,0:T(8,128)(2,1)S(1)}, bf16[1536,1280]{1,0:T(8,128)(2,1)S(1)}) custom-call(bf16[1280,768]{1,0:T(8,128)(2,1)S(1)} %get-tuple-element.13.weighted, bf16[320,1536]{1,0:T(8,128)(2,1)S(1)} %pad_maximum_fusion.refs_0_, bf16[320,1536]{1,0:T(8,128)(2,1)S(1)} %collective-permute-done.12.refs_1_, ...), custom_call_target="tpu_custom_call" | custom-call | tf_op jit(solution)/shard_map/away/pallas_call | solution.py:344
  103.1 6.9 %collective-permute-start.16 = (bf16[1536,768]{1,0:T(8,128)(2,1)S(1)}, bf16[1536,768]{1,0:T(8,128)(2,1)S(1)}, u32[]{:S(2)}, u32[]{:S(2)}) collective-permute-start(bf16[1536,768]{1,0:T(8,128)(2,1)S(1)} %get-tuple-element.16), channel_id=1, source_target_pairs={{0,128},{128,0},{1,129},{129,1},{2,130},{130,2},{3,131},{131,3},{4... | collective-permute-start | bytes 7077896 | tf_op jit(solution)/shard_map/ppermute | solution.py:400
  110.0 4.1 %home.1 = f32[1536,768]{1,0:T(8,128)S(1)} custom-call(bf16[1280,768]{1,0:T(8,128)(2,1)S(1)} %get-tuple-element.12.weighted, bf16[1536,1280]{1,0:T(8,128)(2,1)S(1)} %get-tuple-element.15.rows), custom_call_target="tpu_custom_call" | custom-call | tf_op jit(solution)/shard_map/home/pallas_call | solution.py:370
  114.1 0.1 collective-permute-done.16
  114.2 2.6 %negate_bitcast_fusion = f32[1,1536,768]{2,1,0:T(8,128)} fusion(f32[1536,768]{1,0:T(8,128)S(1)} %home.1, bf16[1536,768]{1,0:T(8,128)(2,1)S(1)} %collective-permute-done.16), kind=kLoop, calls=%fused_computation | loop fusion | flops 3538944 | bytes 11796480 | tf_op jit(solution)/shard_map/neg | solution.py:442
  (3 shorter events, 0.1 us)
Async XLA Ops:
  0.0 5.9 %collective-permute-start.1 = (bf16[4,98304]{1,0:T(4,128)(2,1)}, bf16[4,98304]{1,0:T(4,128)(2,1)S(1)}, u32[]{:S(2)}, u32[]{:S(2)}) collective-permute-start(bf16[4,98304]{1,0:T(4,128)(2,1)} %refs_1_.1), channel_id=1, source_target_pairs={{0,128},{128,0},{1,129},{129,1},{2,130},{130,2},{3,131},{131,3},{4... | collective-permute-start | bytes 2359304 | tf_op jit(solution)/shard_map/ppermute | solution.py:400
  4.7 1.2 %collective-permute-start = (s32[48]{0:T(128)S(1)}, s32[48]{0:T(128)S(1)}, u32[]{:S(2)}, u32[]{:S(2)}) collective-permute-start(s32[48]{0:T(128)S(1)} %pad_add_fusion.mine), channel_id=1, source_target_pairs={{0,128},{128,0},{1,129},{129,1},{2,130},{130,2},{3,131},{131,3},{4... | collective-permute-start | bytes 584 | tf_op jit(solution)/shard_map/ppermute | solution.py:400
  34.3 6.9 %collective-permute-start.11 = (bf16[80,1536]{1,0:T(8,128)(2,1)S(1)}, bf16[80,1536]{1,0:T(8,128)(2,1)S(1)}, u32[]{:S(2)}, u32[]{:S(2)}) collective-permute-start(bf16[80,1536]{1,0:T(8,128)(2,1)S(1)} %pack.1), channel_id=1, source_target_pairs={{0,2},{1,3},{2,0},{3,1},{4,6},{5,7},{6,4},{7,5},{8,10},{9,11},{10,... | collective-permute-start | bytes 737288 | tf_op jit(solution)/shard_map/ppermute | solution.py:392
  37.3 6.9 %collective-permute-start.10 = (bf16[80,1536]{1,0:T(8,128)(2,1)S(1)}, bf16[80,1536]{1,0:T(8,128)(2,1)S(1)}, u32[]{:S(2)}, u32[]{:S(2)}) collective-permute-start(bf16[80,1536]{1,0:T(8,128)(2,1)S(1)} %pack.1), channel_id=1, source_target_pairs={{0,3},{1,0},{2,1},{3,2},{4,7},{5,4},{6,5},{7,6},{8,11},{9,8},{10,9... | collective-permute-start | bytes 737288 | tf_op jit(solution)/shard_map/ppermute | solution.py:392
  38.1 6.6 %collective-permute-start.9 = (bf16[80,1536]{1,0:T(8,128)(2,1)S(1)}, bf16[80,1536]{1,0:T(8,128)(2,1)S(1)}, u32[]{:S(2)}, u32[]{:S(2)}) collective-permute-start(bf16[80,1536]{1,0:T(8,128)(2,1)S(1)} %pack.1), channel_id=1, source_target_pairs={{0,1},{1,2},{2,3},{3,0},{4,5},{5,6},{6,7},{7,4},{8,9},{9,10},{10,1... | collective-permute-start | bytes 737288 | tf_op jit(solution)/shard_map/ppermute | solution.py:392
  44.7 33.9 %collective-permute-start.13 = (bf16[320,1536]{1,0:T(8,128)(2,1)S(1)}, bf16[320,1536]{1,0:T(8,128)(2,1)S(1)}, u32[]{:S(2)}, u32[]{:S(2)}) collective-permute-start(bf16[320,1536]{1,0:T(8,128)(2,1)S(1)} %pad_maximum_fusion.refs_0_), channel_id=1, source_target_pairs={{0,12},{1,13},{2,14},{3,15},{4,0},{5,1},{6,2},{7,3},{8,4},{9,5},{1... | collective-permute-start | bytes 2949128 | tf_op jit(solution)/shard_map/ppermute | solution.py:392
  47.3 32.3 %collective-permute-start.12 = (bf16[320,1536]{1,0:T(8,128)(2,1)S(1)}, bf16[320,1536]{1,0:T(8,128)(2,1)S(1)}, u32[]{:S(2)}, u32[]{:S(2)}) collective-permute-start(bf16[320,1536]{1,0:T(8,128)(2,1)S(1)} %pad_maximum_fusion.refs_0_), channel_id=1, source_target_pairs={{0,4},{1,5},{2,6},{3,7},{4,8},{5,9},{6,10},{7,11},{8,12},{9,13},{1... | collective-permute-start | bytes 2949128 | tf_op jit(solution)/shard_map/ppermute | solution.py:392
  65.8 6.4 %collective-permute-start.2 = (bf16[16,64,128]{2,1,0:T(8,128)(2,1)S(1)}, bf16[16,64,128]{2,1,0:T(8,128)(2,1)S(1)}, u32[]{:S(2)}, u32[]{:S(2)}) collective-permute-start(bf16[16,64,128]{2,1,0:T(8,128)(2,1)S(1)} %all_to_all.11.refs_0_), channel_id=1, source_target_pairs={{0,16},{16,32},{32,48},{48,64},{64,80},{80,96},{96,112},{112,0},{1... | collective-permute-start | bytes 786440 | tf_op jit(solution)/shard_map/ppermute | solution.py:396
  65.8 6.4 %collective-permute-start.6 = (bf16[16,64,128]{2,1,0:T(8,128)(2,1)S(1)}, bf16[16,64,128]{2,1,0:T(8,128)(2,1)S(1)}, u32[]{:S(2)}, u32[]{:S(2)}) collective-permute-start(bf16[16,64,128]{2,1,0:T(8,128)(2,1)S(1)} %all_to_all.11.refs_0_), channel_id=1, source_target_pairs={{0,112},{16,0},{32,16},{48,32},{64,48},{80,64},{96,80},{112,96},{1... | collective-permute-start | bytes 786440 | tf_op jit(solution)/shard_map/ppermute | solution.py:396
  72.2 6.4 %collective-permute-start.3 = (bf16[16,64,128]{2,1,0:T(8,128)(2,1)S(1)}, bf16[16,64,128]{2,1,0:T(8,128)(2,1)S(1)}, u32[]{:S(2)}, u32[]{:S(2)}) collective-permute-start(bf16[16,64,128]{2,1,0:T(8,128)(2,1)S(1)} %collective-permute-done.2.refs_1_), channel_id=1, source_target_pairs={{0,16},{16,32},{32,48},{48,64},{64,80},{80,96},{96,112},{112,0},{1... | collective-permute-start | bytes 786440 | tf_op jit(solution)/shard_map/ppermute | solution.py:396
  72.2 8.3 %collective-permute-start.7 = (bf16[16,64,128]{2,1,0:T(8,128)(2,1)S(1)}, bf16[16,64,128]{2,1,0:T(8,128)(2,1)S(1)}, u32[]{:S(2)}, u32[]{:S(2)}) collective-permute-start(bf16[16,64,128]{2,1,0:T(8,128)(2,1)S(1)} %collective-permute-done.6.refs_5_), channel_id=1, source_target_pairs={{0,112},{16,0},{32,16},{48,32},{64,48},{80,64},{96,80},{112,96},{1... | collective-permute-start | bytes 786440 | tf_op jit(solution)/shard_map/ppermute | solution.py:396
  78.7 6.9 %collective-permute-start.4 = (bf16[16,64,128]{2,1,0:T(8,128)(2,1)S(1)}, bf16[16,64,128]{2,1,0:T(8,128)(2,1)S(1)}, u32[]{:S(2)}, u32[]{:S(2)}) collective-permute-start(bf16[16,64,128]{2,1,0:T(8,128)(2,1)S(1)} %collective-permute-done.3.refs_2_), channel_id=1, source_target_pairs={{0,16},{16,32},{32,48},{48,64},{64,80},{80,96},{96,112},{112,0},{1... | collective-permute-start | bytes 786440 | tf_op jit(solution)/shard_map/ppermute | solution.py:396
  78.7 18.5 %collective-permute-start.15 = (bf16[160,1536]{1,0:T(8,128)(2,1)S(1)}, bf16[160,1536]{1,0:T(8,128)(2,1)S(1)}, u32[]{:S(2)}, u32[]{:S(2)}) collective-permute-start(bf16[160,1536]{1,0:T(8,128)(2,1)S(1)} %slice.9), channel_id=1, source_target_pairs={{0,12},{1,13},{2,14},{3,15},{4,0},{5,1},{6,2},{7,3},{8,4},{9,5},{1... | collective-permute-start | bytes 1474568 | tf_op jit(solution)/shard_map/ppermute | solution.py:392
  79.6 17.6 %collective-permute-start.14 = (bf16[160,1536]{1,0:T(8,128)(2,1)S(1)}, bf16[160,1536]{1,0:T(8,128)(2,1)S(1)}, u32[]{:S(2)}, u32[]{:S(2)}) collective-permute-start(bf16[160,1536]{1,0:T(8,128)(2,1)S(1)} %slice.8), channel_id=1, source_target_pairs={{0,4},{1,5},{2,6},{3,7},{4,8},{5,9},{6,10},{7,11},{8,12},{9,13},{1... | collective-permute-start | bytes 1474568 | tf_op jit(solution)/shard_map/ppermute | solution.py:392
  80.5 6.0 %collective-permute-start.8 = (bf16[16,64,128]{2,1,0:T(8,128)(2,1)S(1)}, bf16[16,64,128]{2,1,0:T(8,128)(2,1)S(1)}, u32[]{:S(2)}, u32[]{:S(2)}) collective-permute-start(bf16[16,64,128]{2,1,0:T(8,128)(2,1)S(1)} %collective-permute-done.7.refs_6_), channel_id=1, source_target_pairs={{0,112},{16,0},{32,16},{48,32},{64,48},{80,64},{96,80},{112,96},{1... | collective-permute-start | bytes 786440 | tf_op jit(solution)/shard_map/ppermute | solution.py:396
  85.6 8.4 %collective-permute-start.5 = (bf16[16,64,128]{2,1,0:T(8,128)(2,1)S(1)}, bf16[16,64,128]{2,1,0:T(8,128)(2,1)S(1)}, u32[]{:S(2)}, u32[]{:S(2)}) collective-permute-start(bf16[16,64,128]{2,1,0:T(8,128)(2,1)S(1)} %collective-permute-done.4.refs_3_), channel_id=1, source_target_pairs={{0,16},{16,32},{32,48},{48,64},{64,80},{80,96},{96,112},{112,0},{1... | collective-permute-start | bytes 786440 | tf_op jit(solution)/shard_map/ppermute | solution.py:396
  103.1 11.1 %collective-permute-start.16 = (bf16[1536,768]{1,0:T(8,128)(2,1)S(1)}, bf16[1536,768]{1,0:T(8,128)(2,1)S(1)}, u32[]{:S(2)}, u32[]{:S(2)}) collective-permute-start(bf16[1536,768]{1,0:T(8,128)(2,1)S(1)} %get-tuple-element.16), channel_id=1, source_target_pairs={{0,128},{128,0},{1,129},{129,1},{2,130},{130,2},{3,131},{131,3},{4... | collective-permute-start | bytes 7077896 | tf_op jit(solution)/shard_map/ppermute | solution.py:400

commit v2 on v1

--- a/solution.py
+++ b/solution.py
@@ -29,7 +29,6 @@
 COLROWS = GCOL * BLOCK + 4
 WIDTH = NP // LANES
 STEP = 512
-ZAROUND = (0, 7, 6, 5, 4, 1, 2, 3)
 F32, BF16 = jnp.float32, jnp.bfloat16
 VMEM = pltpu.VMEM
 SMEM = pltpu.SMEM
@@ -64,13 +63,16 @@
     place, mine, other, *refs,
 ):
     hbm, refs = refs[:10], refs[10:]
-    col_out, row_out, vals, cons, lhs, acc, table_a, table_b, done, lines, row_lines = refs[:11]
-    local, sems = refs[11:21], refs[21]
+    col_out = refs[0]
+    row_outs = refs[1:5]
+    vals, cons, lhs, acc, table_a, table_b, done, lines, row_lines = refs[5:14]
+    local, sems = refs[14:24], refs[24]
     copies = [pltpu.make_async_copy(a, b, sems.at[i]) for i, (a, b) in enumerate(zip(hbm, local))]
     for copy in copies:
         copy.start()
     val, con_mine, con_other, second, third, mix_hi, mix_lo, scale, val_e, con_e = local
     band = place[0] >> 7
+    z = (place[0] >> 4) & 7
     for copy in copies[:3]:
         copy.wait()
 
@@ -92,29 +94,29 @@
     first_count = jnp.where(is_first, mine[2 * SLOTS], other[2 * SLOTS])
     both_count = mine[2 * SLOTS] + other[2 * SLOTS]
     lane = lax.broadcasted_iota(jnp.int32, (1, LANES), 1) & 15
-    gap = jnp.ones((1, LANES), F32)
-    for p in range(HALF):
-        pos = band * HALF + p
-        from_first = pos < first_count
-        slot = jnp.minimum(jnp.where(from_first, pos, pos - first_count), SLOTS - 1)
-        own = from_first == is_first
-        v = jnp.where(own, mine[slot], other[slot])
-        c = jnp.where(own, mine[SLOTS + slot], other[SLOTS + slot])
-        gap = jnp.where(lane == p, con_e[c] - val_e[v], gap)
-        v_line = v * LINES
-        c_line = (jnp.where(own, 0, 4) + (c & 3)) * LINES
-
-        def product(t, carry):
-            made = vals[pl.ds(v_line + t * M1, M1), :] * cons[pl.ds(c_line + t * M1, M1), :]
-            high = made.astype(BF16)
-            where = pl.ds(pl.multiple_of(t * LANES, LANES), LANES)
-            lhs[p * M1 : (p + 1) * M1, where] = high
-            lhs[HALF * M1 + p * M1 : HALF * M1 + (p + 1) * M1, where] = (
-                made - high.astype(F32)
-            ).astype(BF16)
-            return carry
-
-        lax.fori_loop(0, CHUNKS, product, 0, unroll=4)
+    gaps = []
+    for h in range(2):
+        gap = jnp.ones((1, LANES), F32)
+        for p in range(HALF):
+            pos = h * HALF + p
+            from_first = pos < first_count
+            slot = jnp.minimum(jnp.where(from_first, pos, pos - first_count), SLOTS - 1)
+            own = from_first == is_first
+            v = jnp.where(own, mine[slot], other[slot])
+            c = jnp.where(own, mine[SLOTS + slot], other[SLOTS + slot])
+            gap = jnp.where(lane == p, con_e[c] - val_e[v], gap)
+            v_line = v * LINES
+            c_line = (jnp.where(own, 0, 4) + (c & 3)) * LINES
+            top = pos * M1
+
+            def product(t, carry):
+                made = vals[pl.ds(v_line + t * M1, M1), :] * cons[pl.ds(c_line + t * M1, M1), :]
+                where = pl.ds(pl.multiple_of(t * LANES, LANES), LANES)
+                lhs[top : top + M1, where] = made.astype(BF16)
+                return carry
+
+            lax.fori_loop(0, CHUNKS, product, 0, unroll=6)
+        gaps.append(gap)
 
     acc[...] = jnp.zeros_like(acc)
 
@@ -126,9 +128,7 @@
 
     def add(table, k):
         where = pl.ds(pl.multiple_of(k * STEP, STEP), STEP)
-        acc[...] += jnp.dot(
-            lhs[: HALF * M1, where], table[...], preferred_element_type=F32
-        ) + jnp.dot(lhs[HALF * M1 :, where], table[...], preferred_element_type=F32)
+        acc[...] += jnp.dot(lhs[:, where], table[...], preferred_element_type=F32)
 
     last = KP // STEP - 1
     make(table_a, 0)
@@ -141,39 +141,43 @@
         return carry
 
     lax.fori_loop(0, KP // STEP // 2, transform, 0)
-    mid = acc[...]
-    mid_hi = mid.astype(BF16)
-    mid_lo = (mid - mid_hi.astype(F32)).astype(BF16)
-    done[...] = (
-        jnp.dot(mix_hi[...], mid_hi, preferred_element_type=F32)
-        + jnp.dot(mix_hi[...], mid_lo, preferred_element_type=F32)
-        + jnp.dot(mix_lo[...], mid_hi, preferred_element_type=F32)
-    )
-
     at_lane = lax.broadcasted_iota(jnp.int32, (1, LANES), 1)
     frequency = (at_lane >> 4).astype(F32)
-    live = (band * HALF + lane < both_count) & (lane < HALF) & (at_lane < 32)
-    weight = jnp.where(
-        live, 2.0 * gap / (gap * gap + frequency * frequency), 0.0
-    ) * (1.0 / math.sqrt(TOTAL))
-    w_hi = weight.astype(BF16).astype(F32)
-    w_mid = (weight - w_hi).astype(BF16).astype(F32)
-    lines[WIDTH * HALF : WIDTH * HALF + 1, :] = w_hi
-    lines[WIDTH * HALF + 1 : WIDTH * HALF + 2, :] = w_mid
-    lines[WIDTH * HALF + 2 : WIDTH * HALF + 3, :] = weight - w_hi - w_mid
-    lines[WIDTH * HALF + 3 : WIDTH * HALF + 4, :] = jnp.zeros((1, LANES), F32)
-
     norm = 1.0 / math.sqrt(MG)
-    for k in range(N1):
-        block = done[k * 16 : (k + 1) * 16, :] * (scale[k : k + 1, :] * norm)
-        for ch in range(WIDTH):
-            piece = block[:HALF, ch * LANES : (ch + 1) * LANES]
-            lines[ch * HALF : (ch + 1) * HALF, :] = piece
-            at = (k % 2 * WIDTH + ch) * HALF
-            row_lines[at : at + HALF, :] = piece
-        col_out[k] = lines[...].astype(BF16)
-        if k % 2 == 1:
-            row_out[k // 2] = row_lines[...].astype(BF16)
+    for h in range(2):
+        mid = acc[h * HALF * M1 : (h + 1) * HALF * M1, :]
+        mid_hi = mid.astype(BF16)
+        mid_lo = (mid - mid_hi.astype(F32)).astype(BF16)
+        done[...] = (
+            jnp.dot(mix_hi[...], mid_hi, preferred_element_type=F32)
+            + jnp.dot(mix_hi[...], mid_lo, preferred_element_type=F32)
+            + jnp.dot(mix_lo[...], mid_hi, preferred_element_type=F32)
+        )
+        gap = gaps[h]
+        live = (h * HALF + lane < both_count) & (lane < HALF) & (at_lane < 32)
+        weight = jnp.where(
+            live, 2.0 * gap / (gap * gap + frequency * frequency), 0.0
+        ) * (1.0 / math.sqrt(TOTAL))
+        w_hi = weight.astype(BF16).astype(F32)
+        w_mid = (weight - w_hi).astype(BF16).astype(F32)
+        lines[WIDTH * HALF : WIDTH * HALF + 1, :] = w_hi
+        lines[WIDTH * HALF + 1 : WIDTH * HALF + 2, :] = w_mid
+        lines[WIDTH * HALF + 2 : WIDTH * HALF + 3, :] = weight - w_hi - w_mid
+        lines[WIDTH * HALF + 3 : WIDTH * HALF + 4, :] = jnp.zeros((1, LANES), F32)
+        for k in range(N1):
+            block = done[k * 16 : (k + 1) * 16, :] * (scale[k : k + 1, :] * norm)
+            done[k * 16 : (k + 1) * 16, :] = block
+            for ch in range(WIDTH):
+                lines[ch * HALF : (ch + 1) * HALF, :] = block[:HALF, ch * LANES : (ch + 1) * LANES]
+            col_out[k, h] = lines[...].astype(BF16)
+        for i in range(4):
+            target = jnp.where(band == 0, z + i + 1, z - i + GROW) & 7
+            for s in range(2):
+                block = done[pl.ds(pl.multiple_of((2 * target + s) * 16, 16), 16), :]
+                for ch in range(WIDTH):
+                    at = (s * WIDTH + ch) * HALF
+                    row_lines[at : at + HALF, :] = block[:HALF, ch * LANES : (ch + 1) * LANES]
+            row_outs[i][h] = row_lines[...].astype(BF16)
 
 
 def stay(array):
@@ -189,16 +193,16 @@
     return pl.pallas_call(
         density_kernel,
         out_shape=[
-            jax.ShapeDtypeStruct((N1, BLOCK, LANES), BF16),
-            jax.ShapeDtypeStruct((GROW, ROWBLOCK, LANES), BF16),
-        ],
+            jax.ShapeDtypeStruct((N1, 2, BLOCK, LANES), BF16),
+        ]
+        + [jax.ShapeDtypeStruct((2, ROWBLOCK, LANES), BF16)] * 4,
         in_specs=[smem] * 3 + [hbm, hbm, anywhere] + [hbm] * 4 + [anywhere, hbm, hbm],
-        out_specs=[vmem] * 2,
+        out_specs=[vmem] * 5,
         scratch_shapes=[
             VMEM((16 * LINES, LANES), F32),
             VMEM((8 * LINES, LANES), F32),
             VMEM((2 * HALF * M1, KP), BF16),
-            VMEM((HALF * M1, NP), F32),
+            VMEM((2 * HALF * M1, NP), F32),
             VMEM((STEP, NP), BF16),
             VMEM((STEP, NP), BF16),
             VMEM((N1 * 16, NP), F32),
@@ -223,33 +227,31 @@
       stay(mix_hi), stay(mix_lo), scale, stay(val_e), stay(con_e))
 
 
-def pack_kernel(place, blocks, out, spread):
-    z = (place[0] >> 4) & 7
+def pack_kernel(*refs):
+    blocks, out, spread = refs[:4], refs[4], refs[5]
     stride = ROWBLOCK + 4
-    for i in range(GROW):
-        spread[i * stride : i * stride + ROWBLOCK, :] = blocks[(z + ZAROUND[i]) & 7].astype(F32)
+    for v in range(8):
+        spread[v * stride : v * stride + ROWBLOCK, :] = blocks[v // 2][v % 2].astype(F32)
     for ch in range(2 * WIDTH):
         for pp in range(HALF // 2):
-            got = [
-                spread[pl.ds(ch * HALF + 2 * pp + q, GROW, stride=stride), :] for q in range(2)
-            ]
+            got = [spread[pl.ds(ch * HALF + 2 * pp + q, 8, stride=stride), :] for q in range(2)]
             out[pp * 16 : (pp + 1) * 16, ch * LANES : (ch + 1) * LANES] = jnp.concatenate(
                 got, 0
             ).astype(BF16)
 
 
-def pack_call(place, blocks, interpret=False):
+def pack_call(blocks, interpret=False):
     vmem = pl.BlockSpec(memory_space=VMEM)
     return pl.pallas_call(
         pack_kernel,
-        out_shape=jax.ShapeDtypeStruct((GROW * HALF, ROW), BF16),
-        in_specs=[pl.BlockSpec(memory_space=SMEM), vmem],
+        out_shape=jax.ShapeDtypeStruct((8 * HALF, ROW), BF16),
+        in_specs=[vmem] * 4,
         out_specs=vmem,
-        scratch_shapes=[VMEM((GROW * (ROWBLOCK + 4), LANES), F32)],
+        scratch_shapes=[VMEM((8 * (ROWBLOCK + 4), LANES), F32)],
         compiler_params=pltpu.CompilerParams(vmem_limit_bytes=4 << 20),
         interpret=interpret,
         name="pack",
-    )(place, blocks)
+    )(*blocks)
 
 
 def fetch(pieces, rows, sems):
@@ -268,14 +270,23 @@
 
 
 def assemble_kernel(place, *refs):
-    cols = refs[:GROW]
-    away_out, home_out, spread = refs[GROW:]
+    cols = refs[:5]
+    away_out, home_out, spread = refs[5:]
     me = place[0]
     band, y, x = me >> 7, (me >> 2) & 3, me & 3
-    for i, col in enumerate(cols):
-        for q in range(GCOL):
-            at = i * COLROWS + q * BLOCK
-            spread[at : at + BLOCK, :] = col[q].astype(F32)
+
+    def take(first):
+        for i in range(4):
+            def move(q, carry, col=cols[first + i], i=i):
+                for h in range(2):
+                    at = pl.multiple_of((2 * i + h) * COLROWS + q * BLOCK, 4)
+                    spread[pl.ds(at, BLOCK), :] = col[q, h].astype(F32)
+                return carry
+
+            lax.fori_loop(0, GCOL, move, 0, unroll=4)
+
+    pl.when(band == 0)(lambda: take(1))
+    pl.when(band == 1)(lambda: take(0))
 
     def assemble(j, carry):
         outer, inner = around(j >> 2), around(j & 3)
@@ -314,7 +325,7 @@
     return pl.pallas_call(
         assemble_kernel,
         out_shape=[jax.ShapeDtypeStruct((PANEL, NP), BF16)] * 2,
-        in_specs=[pl.BlockSpec(memory_space=SMEM)] + [vmem] * GROW,
+        in_specs=[pl.BlockSpec(memory_space=SMEM)] + [vmem] * 5,
         out_specs=[vmem] * 2,
         scratch_shapes=[VMEM((GROW * COLROWS, LANES), F32)],
         compiler_params=pltpu.CompilerParams(vmem_limit_bytes=14 << 20),
@@ -392,8 +403,12 @@
     return lax.ppermute(array, PLANE, pairs)
 
 
-def up(array, step):
-    return lax.ppermute(array, "grow", [(i, (i + step) % GROW) for i in range(GROW)])
+def along(array, up_by, down_by):
+    pairs = []
+    for band, step in ((0, up_by), (1, -down_by if down_by is not None else None)):
+        if step is not None:
+            pairs += [(band * GROW + z, band * GROW + (z + step) % GROW) for z in range(GROW)]
+    return lax.ppermute(array, ("band", "grow"), pairs)
 
 
 def swap(array):
@@ -414,28 +429,26 @@
     other_con = swap(conduction_orbitals)
     other_meta = swap(meta)
     scale = coulomb_root.reshape(N1, NP)
-    col, row = density_call(
+    col, *rows = density_call(
         place, meta, other_meta, valence_energy, conduction_energy,
         valence_orbitals, conduction_orbitals, other_con, scale,
     )
-    return exchange(place, col, row)
-
-
-def exchange(place, col, row):
-    row = lax.all_to_all(row, "grow", 0, 0, tiled=True)
+    return exchange(place, col, rows)
+
+
+def exchange(place, col, rows):
+    rows = [along(rows[i], i + 1, i) for i in range(4)]
     col = lax.all_to_all(col, ("gcol_0", "gcol_1"), 0, 0, tiled=True)
-    row = pack_call(place, row)
-    ups, downs = [col], [col]
-    for _ in range(1, 5):
-        ups.append(up(ups[-1], 1))
-    for _ in range(1, 4):
-        downs.append(up(downs[-1], -1))
+    row = pack_call(rows)
+    ring = [col]
+    for i in range(1, 5):
+        ring.append(along(ring[-1], 1, 1 if i < 4 else None))
     below, above, far = turned(row, 0, 1), turned(row, 0, -1), turned(row, 0, 2)
     line = jnp.concatenate([row, below, above, far], 0)
     half = line.shape[0] // 2
     below, above = turned(line, 1, 1), turned(line, 1, -1)
     far_a, far_b = turned(below[:half], 1, 1), turned(above[half:], 1, -1)
-    weighted_away, weighted_home = assemble_call(place, ups + downs[1:])
+    weighted_away, weighted_home = assemble_call(place, ring)
     away, turned_rows = away_call(weighted_away, [line, below, above, far_a, far_b])
     received = swap(away)
     home = home_call(weighted_home, turned_rows)

time: 119 us -> 112 us (0.941); the launches traced: 117 us -> 112 us
  blocking collectives: 36.3 us -> 15.7 us
  starting transfers between devices: 27 us -> 35.7 us
  waiting for transfers between devices: 24.5 us -> 29.9 us
  Pallas kernels: 23.9 us -> 25.2 us
    all_to_all x1 -> x0, blocking collectives: 17.8 us -> none  [exchange(): row = lax.all_to_all(row, 'grow', 0, 0, tiled=True)]
    ppermute x7, waiting for transfers between devices: 5.87 us -> 15.9 us  [turned(): return lax.ppermute(array, PLANE, pairs)]
    ppermute x7 -> x8, starting transfers between devices: 8.03 us -> 14.1 us  [along(): return lax.ppermute(array, ('band', 'grow'), pairs)]
    ppermute x3, starting transfers between devices: 10.1 us -> 15.4 us  [swap(): return lax.ppermute(array, 'band', [(0, 1), (1, 0)])]
    ppermute x7 -> x8, waiting for transfers between devices: 18.2 us -> 13.6 us  [along(): return lax.ppermute(array, ('band', 'grow'), pairs)]
    all_to_all x1, blocking collectives: 18.5 us -> 15.7 us  [exchange(): col = lax.all_to_all(col, ('gcol_0', 'gcol_1'), 0, 0, tiled=True)]
    ppermute x7, starting transfers between devices: 8.82 us -> 6.21 us  [turned(): return lax.ppermute(array, PLANE, pairs)]
    pallas_call x2, Pallas kernels: 10.7 us -> 11.9 us  [the longest x1 11.9 us: density_call(): pl.pallas_call(density_kernel, out_shape=[jax.ShapeDtypeStruct((N1, 2, BL...]
  transfers between devices with their start and end apart: 17 -> 18, of which waited for: 10 -> 12; matrix products, arithmetic and copies ran while one was open for 1% -> 2% of each run, Pallas kernels for 6% -> 7%
where the time goes in v2:
time: 112 us
  starting transfers between devices  35.7 us (32%)
  waiting for transfers between devices  29.9 us (27%)
  Pallas kernels  25.2 us (22%)
  blocking collectives  15.7 us (14%)
  other arithmetic  2.79 us (2%)
  local copies, waits for them, and re-layouts  1.64 us (1%)
    ppermute x7, waiting for transfers between devices, turned(): return lax.ppermute(array, PLANE, pairs)  15.9 us
    all_to_all x1, blocking collectives, exchange(): col = lax.all_to_all(col, ('gcol_0', 'gcol_1'), 0, 0, tiled=True)  15.7 us
    ppermute x3, starting transfers between devices, swap(): return lax.ppermute(array, 'band', [(0, 1), (1, 0)])  15.4 us
    ppermute x8, starting transfers between devices, along(): return lax.ppermute(array, ('band', 'grow'), pairs)  14.1 us
    ppermute x8, waiting for transfers between devices, along(): return lax.ppermute(array, ('band', 'grow'), pairs)  13.6 us
    pallas_call x1, Pallas kernels, density_call(): pl.pallas_call(density_kernel, out_shape=[jax.ShapeDtypeStruct((N1, 2, BL...  11.9 us
    ppermute x7, starting transfers between devices, turned(): return lax.ppermute(array, PLANE, pairs)  6.21 us
    pallas_call x1, Pallas kernels, away_call(): pl.pallas_call(away_kernel, out_shape=(jax.ShapeDtypeStruct((ROW, NP), BF...  5.94 us
  transfers between devices with their start and end apart: 18, of which 12 were waited for; matrix products, arithmetic and copies ran while one was open for 2% of the time, Pallas kernels for 7%

profile of v2, /device:TPU:1, one launch (start us, length us, event | category | flops | bytes accessed | tf_op | source)
XLA Modules:
  0.0 111.6 jit_solution(16397001724790977423)
XLA Ops:
  0.0 3.2 %collective-permute-start.1 = (bf16[4,98304]{1,0:T(4,128)(2,1)}, bf16[4,98304]{1,0:T(4,128)(2,1)S(1)}, u32[]{:S(2)}, u32[]{:S(2)}) collective-permute-start(bf16[4,98304]{1,0:T(4,128)(2,1)} %refs_1_.1), channel_id=1, source_target_pairs={{0,128},{128,0},{1,129},{129,1},{2,130},{130,2},{3,131},{131,3},{4... | collective-permute-start | bytes 2359304 | tf_op jit(solution)/shard_map/ppermute | solution.py:415
  3.9 0.8 reshape.11
  4.6 0.1 pad_add_fusion.mine
  4.7 0.0 collective-permute-start
  4.7 0.8 reshape.12.refs_7_
  5.6 0.3 collective-permute-done.other
  5.9 0.0 collective-permute-done.1.refs_2_
  5.9 11.9 %density.1 = (bf16[16,2,64,128]{3,2,1,0:T(8,128)(2,1)S(1)}, bf16[2,120,128]{2,1,0:T(8,128)(2,1)S(1)}, bf16[2,120,128]{2,1,0:T(8,128)(2,1)S(1)}, bf16[2,120,128]{2,1,0:T(8,128)(2,1)S(1)}, bf16[2,120,128]{2,1,0:T(8,128)(2,1)S(1)}) custom-call(s32[1]{0:T(128)} %bitcast.place, s32[48]{0:T(128)S(1)} %pad_add_fusion.mine, s32[48]{0:T(128)S(1)} %collective-permute-done.other, ...), custom_call_target="tpu_custom_call" | custom-call | tf_op jit(solution)/shard_map/density/pallas_call | solution.py:193
  17.8 15.7 %all_to_all.5.refs_0_ = bf16[16,2,64,128]{3,2,1,0:T(8,128)(2,1)S(1)} all-to-all(bf16[16,2,64,128]{3,2,1,0:T(8,128)(2,1)S(1)} %get-tuple-element.14), channel_id=1, replica_groups=mesh['band'=2,'grow'=8,'gcol_0'=4,'gcol_1'=4] {'gcol_0','gcol_1'}, dimensions={0} | all-to-all | bytes 1048576 | tf_op jit(solution)/shard_map/all_to_all | solution.py:441
  33.4 5.7 %collective-permute-start.2 = (bf16[16,2,64,128]{3,2,1,0:T(8,128)(2,1)S(1)}, bf16[16,2,64,128]{3,2,1,0:T(8,128)(2,1)S(1)}, u32[]{:S(2)}, u32[]{:S(2)}) collective-permute-start(bf16[16,2,64,128]{3,2,1,0:T(8,128)(2,1)S(1)} %all_to_all.5.refs_0_), channel_id=1, source_target_pairs={{0,16},{16,32},{32,48},{48,64},{64,80},{80,96},{96,112},{112,0},{1... | collective-permute-start | bytes 1572872 | tf_op jit(solution)/shard_map/ppermute | solution.py:411
  39.1 0.7 collective-permute-start.6
  39.8 0.6 collective-permute-start.7
  40.4 1.3 %collective-permute-start.8 = (bf16[2,120,128]{2,1,0:T(8,128)(2,1)S(1)}, bf16[2,120,128]{2,1,0:T(8,128)(2,1)S(1)}, u32[]{:S(2)}, u32[]{:S(2)}) collective-permute-start(bf16[2,120,128]{2,1,0:T(8,128)(2,1)S(1)} %get-tuple-element.19), channel_id=1, source_target_pairs={{0,48},{16,64},{32,80},{48,96},{64,112},{80,0},{96,16},{112,32},{1... | collective-permute-start | bytes 184328 | tf_op jit(solution)/shard_map/ppermute | solution.py:411
  41.7 0.0 collective-permute-start.9
  41.7 0.0 collective-permute-done.6.refs_0_
  41.7 6.1 %collective-permute-done.7.refs_1_ = bf16[2,120,128]{2,1,0:T(8,128)(2,1)S(1)} collective-permute-done((bf16[2,120,128]{2,1,0:T(8,128)(2,1)S(1)}, bf16[2,120,128]{2,1,0:T(8,128)(2,1)S(1)}, u32[]{:S(2)}, u32[]{:S(2)}) %collective-permute-start.7) | collective-permute-done | bytes 61472 | tf_op jit(solution)/shard_map/ppermute | solution.py:411
  47.9 0.7 collective-permute-done.8.refs_2_
  48.5 0.7 collective-permute-done.9.refs_3_
  49.2 0.1 pack.1
  49.3 0.7 collective-permute-start.12
  49.9 1.2 %collective-permute-start.11 = (bf16[80,1536]{1,0:T(8,128)(2,1)S(1)}, bf16[80,1536]{1,0:T(8,128)(2,1)S(1)}, u32[]{:S(2)}, u32[]{:S(2)}) collective-permute-start(bf16[80,1536]{1,0:T(8,128)(2,1)S(1)} %pack.1), channel_id=1, source_target_pairs={{0,3},{1,0},{2,1},{3,2},{4,7},{5,4},{6,5},{7,6},{8,11},{9,8},{10,9... | collective-permute-start | bytes 737288 | tf_op jit(solution)/shard_map/ppermute | solution.py:403
  51.1 0.3 collective-permute-start.10
  51.4 0.0 collective-permute-done.2.refs_1_
  51.4 1.9 %collective-permute-start.3 = (bf16[16,2,64,128]{3,2,1,0:T(8,128)(2,1)S(1)}, bf16[16,2,64,128]{3,2,1,0:T(8,128)(2,1)S(1)}, u32[]{:S(2)}, u32[]{:S(2)}) collective-permute-start(bf16[16,2,64,128]{3,2,1,0:T(8,128)(2,1)S(1)} %collective-permute-done.2.refs_1_), channel_id=1, source_target_pairs={{0,16},{16,32},{32,48},{48,64},{64,80},{80,96},{96,112},{112,0},{1... | collective-permute-start | bytes 1572872 | tf_op jit(solution)/shard_map/ppermute | solution.py:411
  53.3 2.9 %collective-permute-done.12 = bf16[80,1536]{1,0:T(8,128)(2,1)S(1)} collective-permute-done((bf16[80,1536]{1,0:T(8,128)(2,1)S(1)}, bf16[80,1536]{1,0:T(8,128)(2,1)S(1)}, u32[]{:S(2)}, u32[]{:S(2)}) %collective-permute-start.12) | collective-permute-done | bytes 245792 | tf_op jit(solution)/shard_map/ppermute | solution.py:403
  56.2 0.5 collective-permute-done.11
  56.7 1.8 %collective-permute-done.10 = bf16[80,1536]{1,0:T(8,128)(2,1)S(1)} collective-permute-done((bf16[80,1536]{1,0:T(8,128)(2,1)S(1)}, bf16[80,1536]{1,0:T(8,128)(2,1)S(1)}, u32[]{:S(2)}, u32[]{:S(2)}) %collective-permute-start.10) | collective-permute-done | bytes 245792 | tf_op jit(solution)/shard_map/ppermute | solution.py:403
  58.5 0.1 pad_maximum_fusion.refs_0_
  58.6 0.1 collective-permute-start.14
  58.7 1.5 %collective-permute-start.13 = (bf16[320,1536]{1,0:T(8,128)(2,1)S(1)}, bf16[320,1536]{1,0:T(8,128)(2,1)S(1)}, u32[]{:S(2)}, u32[]{:S(2)}) collective-permute-start(bf16[320,1536]{1,0:T(8,128)(2,1)S(1)} %pad_maximum_fusion.refs_0_), channel_id=1, source_target_pairs={{0,4},{1,5},{2,6},{3,7},{4,8},{5,9},{6,10},{7,11},{8,12},{9,13},{1... | collective-permute-start | bytes 2949128 | tf_op jit(solution)/shard_map/ppermute | solution.py:403
  60.1 0.0 collective-permute-done.3.refs_2_
  60.1 3.1 %collective-permute-start.4 = (bf16[16,2,64,128]{3,2,1,0:T(8,128)(2,1)S(1)}, bf16[16,2,64,128]{3,2,1,0:T(8,128)(2,1)S(1)}, u32[]{:S(2)}, u32[]{:S(2)}) collective-permute-start(bf16[16,2,64,128]{3,2,1,0:T(8,128)(2,1)S(1)} %collective-permute-done.3.refs_2_), channel_id=1, source_target_pairs={{0,16},{16,32},{32,48},{48,64},{64,80},{80,96},{96,112},{112,0},{1... | collective-permute-start | bytes 1572872 | tf_op jit(solution)/shard_map/ppermute | solution.py:411
  63.3 6.1 %collective-permute-done.4.refs_3_ = bf16[16,2,64,128]{3,2,1,0:T(8,128)(2,1)S(1)} collective-permute-done((bf16[16,2,64,128]{3,2,1,0:T(8,128)(2,1)S(1)}, bf16[16,2,64,128]{3,2,1,0:T(8,128)(2,1)S(1)}, u32[]{:S(2)}, u32[]{:S(2)}) %collective-permute-start.4) | collective-permute-done | bytes 524320 | tf_op jit(solution)/shard_map/ppermute | solution.py:411
  69.4 0.7 collective-permute-start.5
  70.1 5.1 %collective-permute-done.14.refs_2_ = bf16[320,1536]{1,0:T(8,128)(2,1)S(1)} collective-permute-done((bf16[320,1536]{1,0:T(8,128)(2,1)S(1)}, bf16[320,1536]{1,0:T(8,128)(2,1)S(1)}, u32[]{:S(2)}, u32[]{:S(2)}) %collective-permute-start.14) | collective-permute-done | bytes 983072 | tf_op jit(solution)/shard_map/ppermute | solution.py:403
  75.3 2.5 %collective-permute-start.16 = (bf16[160,1536]{1,0:T(8,128)(2,1)S(1)}, bf16[160,1536]{1,0:T(8,128)(2,1)S(1)}, u32[]{:S(2)}, u32[]{:S(2)}) collective-permute-start(bf16[160,1536]{1,0:T(8,128)(2,1)S(1)} %slice.9), channel_id=1, source_target_pairs={{0,12},{1,13},{2,14},{3,15},{4,0},{5,1},{6,2},{7,3},{8,4},{9,5},{1... | collective-permute-start | bytes 1474568 | tf_op jit(solution)/shard_map/ppermute | solution.py:403
  77.7 0.0 collective-permute-done.13.refs_1_
  77.8 0.1 collective-permute-start.15
  77.9 0.0 collective-permute-done.5.refs_4_
  77.9 3.3 %assemble.1 = (bf16[1280,768]{1,0:T(8,128)(2,1)S(1)}, bf16[1280,768]{1,0:T(8,128)(2,1)S(1)}) custom-call(s32[1]{0:T(128)} %bitcast.place, bf16[16,2,64,128]{3,2,1,0:T(8,128)(2,1)S(1)} %all_to_all.5.refs_0_, bf16[16,2,64,128]{3,2,1,0:T(8,128)(2,1)S(1)} %collective-permute-done.2.refs_1_, bf16[16,2,64,128]{3,2,1,0:T(8,128)(2,1)S(1)} %collective-permute-done.3.refs_2_, ...), custom_call_target="tpu_custom_call" | custom-call | tf_op jit(solution)/shard_map/assemble/pallas_call | solution.py:325
  81.1 2.5 %collective-permute-done.16.refs_4_ = bf16[160,1536]{1,0:T(8,128)(2,1)S(1)} collective-permute-done((bf16[160,1536]{1,0:T(8,128)(2,1)S(1)}, bf16[160,1536]{1,0:T(8,128)(2,1)S(1)}, u32[]{:S(2)}, u32[]{:S(2)}) %collective-permute-start.16) | collective-permute-done | bytes 491552 | tf_op jit(solution)/shard_map/ppermute | solution.py:403
  83.7 3.0 %collective-permute-done.15.refs_3_ = bf16[160,1536]{1,0:T(8,128)(2,1)S(1)} collective-permute-done((bf16[160,1536]{1,0:T(8,128)(2,1)S(1)}, bf16[160,1536]{1,0:T(8,128)(2,1)S(1)}, u32[]{:S(2)}, u32[]{:S(2)}) %collective-permute-start.15) | collective-permute-done | bytes 491552 | tf_op jit(solution)/shard_map/ppermute | solution.py:403
  86.7 5.9 %away.1 = (bf16[1536,768]{1,0:T(8,128)(2,1)S(1)}, bf16[1536,1280]{1,0:T(8,128)(2,1)S(1)}) custom-call(bf16[1280,768]{1,0:T(8,128)(2,1)S(1)} %get-tuple-element.16.weighted, bf16[320,1536]{1,0:T(8,128)(2,1)S(1)} %pad_maximum_fusion.refs_0_, bf16[320,1536]{1,0:T(8,128)(2,1)S(1)} %collective-permute-done.13.refs_1_, ...), custom_call_target="tpu_custom_call" | custom-call | tf_op jit(solution)/shard_map/away/pallas_call | solution.py:355
  92.7 12.1 %collective-permute-start.17 = (bf16[1536,768]{1,0:T(8,128)(2,1)S(1)}, bf16[1536,768]{1,0:T(8,128)(2,1)S(1)}, u32[]{:S(2)}, u32[]{:S(2)}) collective-permute-start(bf16[1536,768]{1,0:T(8,128)(2,1)S(1)} %get-tuple-element.22), channel_id=1, source_target_pairs={{0,128},{128,0},{1,129},{129,1},{2,130},{130,2},{3,131},{131,3},{4... | collective-permute-start | bytes 7077896 | tf_op jit(solution)/shard_map/ppermute | solution.py:415
  104.8 4.1 %home.1 = f32[1536,768]{1,0:T(8,128)S(1)} custom-call(bf16[1280,768]{1,0:T(8,128)(2,1)S(1)} %get-tuple-element.15.weighted, bf16[1536,1280]{1,0:T(8,128)(2,1)S(1)} %get-tuple-element.21.rows), custom_call_target="tpu_custom_call" | custom-call | tf_op jit(solution)/shard_map/home/pallas_call | solution.py:381
  108.9 0.1 collective-permute-done.17
  109.0 2.6 %negate_bitcast_fusion = f32[1,1536,768]{2,1,0:T(8,128)} fusion(f32[1536,768]{1,0:T(8,128)S(1)} %home.1, bf16[1536,768]{1,0:T(8,128)(2,1)S(1)} %collective-permute-done.17), kind=kLoop, calls=%fused_computation | loop fusion | flops 3538944 | bytes 11796480 | tf_op jit(solution)/shard_map/neg | solution.py:455
  (3 shorter events, 0.1 us)
Async XLA Ops:
  0.0 5.9 %collective-permute-start.1 = (bf16[4,98304]{1,0:T(4,128)(2,1)}, bf16[4,98304]{1,0:T(4,128)(2,1)S(1)}, u32[]{:S(2)}, u32[]{:S(2)}) collective-permute-start(bf16[4,98304]{1,0:T(4,128)(2,1)} %refs_1_.1), channel_id=1, source_target_pairs={{0,128},{128,0},{1,129},{129,1},{2,130},{130,2},{3,131},{131,3},{4... | collective-permute-start | bytes 2359304 | tf_op jit(solution)/shard_map/ppermute | solution.py:415
  4.7 1.2 %collective-permute-start = (s32[48]{0:T(128)S(1)}, s32[48]{0:T(128)S(1)}, u32[]{:S(2)}, u32[]{:S(2)}) collective-permute-start(s32[48]{0:T(128)S(1)} %pad_add_fusion.mine), channel_id=1, source_target_pairs={{0,128},{128,0},{1,129},{129,1},{2,130},{130,2},{3,131},{131,3},{4... | collective-permute-start | bytes 584 | tf_op jit(solution)/shard_map/ppermute | solution.py:415
  33.4 18.0 %collective-permute-start.2 = (bf16[16,2,64,128]{3,2,1,0:T(8,128)(2,1)S(1)}, bf16[16,2,64,128]{3,2,1,0:T(8,128)(2,1)S(1)}, u32[]{:S(2)}, u32[]{:S(2)}) collective-permute-start(bf16[16,2,64,128]{3,2,1,0:T(8,128)(2,1)S(1)} %all_to_all.5.refs_0_), channel_id=1, source_target_pairs={{0,16},{16,32},{32,48},{48,64},{64,80},{80,96},{96,112},{112,0},{1... | collective-permute-start | bytes 1572872 | tf_op jit(solution)/shard_map/ppermute | solution.py:411
  39.1 2.6 %collective-permute-start.6 = (bf16[2,120,128]{2,1,0:T(8,128)(2,1)S(1)}, bf16[2,120,128]{2,1,0:T(8,128)(2,1)S(1)}, u32[]{:S(2)}, u32[]{:S(2)}) collective-permute-start(bf16[2,120,128]{2,1,0:T(8,128)(2,1)S(1)} %get-tuple-element.17), channel_id=1, source_target_pairs={{0,16},{16,32},{32,48},{48,64},{64,80},{80,96},{96,112},{112,0},{1... | collective-permute-start | bytes 184328 | tf_op jit(solution)/shard_map/ppermute | solution.py:411
  39.8 8.1 %collective-permute-start.7 = (bf16[2,120,128]{2,1,0:T(8,128)(2,1)S(1)}, bf16[2,120,128]{2,1,0:T(8,128)(2,1)S(1)}, u32[]{:S(2)}, u32[]{:S(2)}) collective-permute-start(bf16[2,120,128]{2,1,0:T(8,128)(2,1)S(1)} %get-tuple-element.18), channel_id=1, source_target_pairs={{0,32},{16,48},{32,64},{48,80},{64,96},{80,112},{96,0},{112,16},{1... | collective-permute-start | bytes 184328 | tf_op jit(solution)/shard_map/ppermute | solution.py:411
  40.4 8.1 %collective-permute-start.8 = (bf16[2,120,128]{2,1,0:T(8,128)(2,1)S(1)}, bf16[2,120,128]{2,1,0:T(8,128)(2,1)S(1)}, u32[]{:S(2)}, u32[]{:S(2)}) collective-permute-start(bf16[2,120,128]{2,1,0:T(8,128)(2,1)S(1)} %get-tuple-element.19), channel_id=1, source_target_pairs={{0,48},{16,64},{32,80},{48,96},{64,112},{80,0},{96,16},{112,32},{1... | collective-permute-start | bytes 184328 | tf_op jit(solution)/shard_map/ppermute | solution.py:411
  41.7 7.5 %collective-permute-start.9 = (bf16[2,120,128]{2,1,0:T(8,128)(2,1)S(1)}, bf16[2,120,128]{2,1,0:T(8,128)(2,1)S(1)}, u32[]{:S(2)}, u32[]{:S(2)}) collective-permute-start(bf16[2,120,128]{2,1,0:T(8,128)(2,1)S(1)} %get-tuple-element.20), channel_id=1, source_target_pairs={{0,64},{16,80},{32,96},{48,112},{64,0},{80,16},{96,32},{112,48},{1... | collective-permute-start | bytes 184328 | tf_op jit(solution)/shard_map/ppermute | solution.py:411
  49.3 6.9 %collective-permute-start.12 = (bf16[80,1536]{1,0:T(8,128)(2,1)S(1)}, bf16[80,1536]{1,0:T(8,128)(2,1)S(1)}, u32[]{:S(2)}, u32[]{:S(2)}) collective-permute-start(bf16[80,1536]{1,0:T(8,128)(2,1)S(1)} %pack.1), channel_id=1, source_target_pairs={{0,2},{1,3},{2,0},{3,1},{4,6},{5,7},{6,4},{7,5},{8,10},{9,11},{10,... | collective-permute-start | bytes 737288 | tf_op jit(solution)/shard_map/ppermute | solution.py:403
  49.9 6.8 %collective-permute-start.11 = (bf16[80,1536]{1,0:T(8,128)(2,1)S(1)}, bf16[80,1536]{1,0:T(8,128)(2,1)S(1)}, u32[]{:S(2)}, u32[]{:S(2)}) collective-permute-start(bf16[80,1536]{1,0:T(8,128)(2,1)S(1)} %pack.1), channel_id=1, source_target_pairs={{0,3},{1,0},{2,1},{3,2},{4,7},{5,4},{6,5},{7,6},{8,11},{9,8},{10,9... | collective-permute-start | bytes 737288 | tf_op jit(solution)/shard_map/ppermute | solution.py:403
  51.1 7.4 %collective-permute-start.10 = (bf16[80,1536]{1,0:T(8,128)(2,1)S(1)}, bf16[80,1536]{1,0:T(8,128)(2,1)S(1)}, u32[]{:S(2)}, u32[]{:S(2)}) collective-permute-start(bf16[80,1536]{1,0:T(8,128)(2,1)S(1)} %pack.1), channel_id=1, source_target_pairs={{0,1},{1,2},{2,3},{3,0},{4,5},{5,6},{6,7},{7,4},{8,9},{9,10},{10,1... | collective-permute-start | bytes 737288 | tf_op jit(solution)/shard_map/ppermute | solution.py:403
  51.4 8.8 %collective-permute-start.3 = (bf16[16,2,64,128]{3,2,1,0:T(8,128)(2,1)S(1)}, bf16[16,2,64,128]{3,2,1,0:T(8,128)(2,1)S(1)}, u32[]{:S(2)}, u32[]{:S(2)}) collective-permute-start(bf16[16,2,64,128]{3,2,1,0:T(8,128)(2,1)S(1)} %collective-permute-done.2.refs_1_), channel_id=1, source_target_pairs={{0,16},{16,32},{32,48},{48,64},{64,80},{80,96},{96,112},{112,0},{1... | collective-permute-start | bytes 1572872 | tf_op jit(solution)/shard_map/ppermute | solution.py:411
  58.6 16.6 %collective-permute-start.14 = (bf16[320,1536]{1,0:T(8,128)(2,1)S(1)}, bf16[320,1536]{1,0:T(8,128)(2,1)S(1)}, u32[]{:S(2)}, u32[]{:S(2)}) collective-permute-start(bf16[320,1536]{1,0:T(8,128)(2,1)S(1)} %pad_maximum_fusion.refs_0_), channel_id=1, source_target_pairs={{0,12},{1,13},{2,14},{3,15},{4,0},{5,1},{6,2},{7,3},{8,4},{9,5},{1... | collective-permute-start | bytes 2949128 | tf_op jit(solution)/shard_map/ppermute | solution.py:403
  58.7 19.0 %collective-permute-start.13 = (bf16[320,1536]{1,0:T(8,128)(2,1)S(1)}, bf16[320,1536]{1,0:T(8,128)(2,1)S(1)}, u32[]{:S(2)}, u32[]{:S(2)}) collective-permute-start(bf16[320,1536]{1,0:T(8,128)(2,1)S(1)} %pad_maximum_fusion.refs_0_), channel_id=1, source_target_pairs={{0,4},{1,5},{2,6},{3,7},{4,8},{5,9},{6,10},{7,11},{8,12},{9,13},{1... | collective-permute-start | bytes 2949128 | tf_op jit(solution)/shard_map/ppermute | solution.py:403
  60.1 9.3 %collective-permute-start.4 = (bf16[16,2,64,128]{3,2,1,0:T(8,128)(2,1)S(1)}, bf16[16,2,64,128]{3,2,1,0:T(8,128)(2,1)S(1)}, u32[]{:S(2)}, u32[]{:S(2)}) collective-permute-start(bf16[16,2,64,128]{3,2,1,0:T(8,128)(2,1)S(1)} %collective-permute-done.3.refs_2_), channel_id=1, source_target_pairs={{0,16},{16,32},{32,48},{48,64},{64,80},{80,96},{96,112},{112,0},{1... | collective-permute-start | bytes 1572872 | tf_op jit(solution)/shard_map/ppermute | solution.py:411
  69.4 8.4 %collective-permute-start.5 = (bf16[16,2,64,128]{3,2,1,0:T(8,128)(2,1)S(1)}, bf16[16,2,64,128]{3,2,1,0:T(8,128)(2,1)S(1)}, u32[]{:S(2)}, u32[]{:S(2)}) collective-permute-start(bf16[16,2,64,128]{3,2,1,0:T(8,128)(2,1)S(1)} %collective-permute-done.4.refs_3_), channel_id=1, source_target_pairs={{0,16},{16,32},{32,48},{48,64},{64,80},{80,96},{96,112},{112,0},{1... | collective-permute-start | bytes 1572872 | tf_op jit(solution)/shard_map/ppermute | solution.py:411
  75.3 8.4 %collective-permute-start.16 = (bf16[160,1536]{1,0:T(8,128)(2,1)S(1)}, bf16[160,1536]{1,0:T(8,128)(2,1)S(1)}, u32[]{:S(2)}, u32[]{:S(2)}) collective-permute-start(bf16[160,1536]{1,0:T(8,128)(2,1)S(1)} %slice.9), channel_id=1, source_target_pairs={{0,12},{1,13},{2,14},{3,15},{4,0},{5,1},{6,2},{7,3},{8,4},{9,5},{1... | collective-permute-start | bytes 1474568 | tf_op jit(solution)/shard_map/ppermute | solution.py:403
  77.8 9.0 %collective-permute-start.15 = (bf16[160,1536]{1,0:T(8,128)(2,1)S(1)}, bf16[160,1536]{1,0:T(8,128)(2,1)S(1)}, u32[]{:S(2)}, u32[]{:S(2)}) collective-permute-start(bf16[160,1536]{1,0:T(8,128)(2,1)S(1)} %slice.8), channel_id=1, source_target_pairs={{0,4},{1,5},{2,6},{3,7},{4,8},{5,9},{6,10},{7,11},{8,12},{9,13},{1... | collective-permute-start | bytes 1474568 | tf_op jit(solution)/shard_map/ppermute | solution.py:403
  92.7 16.3 %collective-permute-start.17 = (bf16[1536,768]{1,0:T(8,128)(2,1)S(1)}, bf16[1536,768]{1,0:T(8,128)(2,1)S(1)}, u32[]{:S(2)}, u32[]{:S(2)}) collective-permute-start(bf16[1536,768]{1,0:T(8,128)(2,1)S(1)} %get-tuple-element.22), channel_id=1, source_target_pairs={{0,128},{128,0},{1,129},{129,1},{2,130},{130,2},{3,131},{131,3},{4... | collective-permute-start | bytes 7077896 | tf_op jit(solution)/shard_map/ppermute | solution.py:415

commit v3 on v2

--- a/solution.py
+++ b/solution.py
@@ -73,6 +73,7 @@
     val, con_mine, con_other, second, third, mix_hi, mix_lo, scale, val_e, con_e = local
     band = place[0] >> 7
     z = (place[0] >> 4) & 7
+    skip = jnp.where((band == 0) == ((place[0] & 15) < 8), 1, 0)
     for copy in copies[:3]:
         copy.wait()
 
@@ -171,7 +172,7 @@
                 lines[ch * HALF : (ch + 1) * HALF, :] = block[:HALF, ch * LANES : (ch + 1) * LANES]
             col_out[k, h] = lines[...].astype(BF16)
         for i in range(4):
-            target = jnp.where(band == 0, z + i + 1, z - i + GROW) & 7
+            target = jnp.where(band == 0, z + i + skip, z - i - skip + GROW) & 7
             for s in range(2):
                 block = done[pl.ds(pl.multiple_of((2 * target + s) * 16, 16), 16), :]
                 for ch in range(WIDTH):
@@ -270,23 +271,28 @@
 
 
 def assemble_kernel(place, *refs):
-    cols = refs[:5]
-    away_out, home_out, spread = refs[5:]
+    cols = refs[:10]
+    away_out, home_out, spread = refs[10:]
     me = place[0]
     band, y, x = me >> 7, (me >> 2) & 3, me & 3
 
-    def take(first):
+    def take(part, first):
         for i in range(4):
-            def move(q, carry, col=cols[first + i], i=i):
+            col = cols[part * 5 + first + i]
+            for q in range(GCOL // 2):
                 for h in range(2):
-                    at = pl.multiple_of((2 * i + h) * COLROWS + q * BLOCK, 4)
-                    spread[pl.ds(at, BLOCK), :] = col[q, h].astype(F32)
-                return carry
-
-            lax.fori_loop(0, GCOL, move, 0, unroll=4)
-
-    pl.when(band == 0)(lambda: take(1))
-    pl.when(band == 1)(lambda: take(0))
+                    at = (2 * i + h) * COLROWS + (part * 8 + q) * BLOCK
+                    spread[at : at + BLOCK, :] = col[q, h].astype(F32)
+
+    @pl.when(band == 0)
+    def _():
+        take(0, 1)
+        take(1, 0)
+
+    @pl.when(band == 1)
+    def _():
+        take(0, 0)
+        take(1, 1)
 
     def assemble(j, carry):
         outer, inner = around(j >> 2), around(j & 3)
@@ -325,7 +331,7 @@
     return pl.pallas_call(
         assemble_kernel,
         out_shape=[jax.ShapeDtypeStruct((PANEL, NP), BF16)] * 2,
-        in_specs=[pl.BlockSpec(memory_space=SMEM)] + [vmem] * 5,
+        in_specs=[pl.BlockSpec(memory_space=SMEM)] + [vmem] * 10,
         out_specs=[vmem] * 2,
         scratch_shapes=[VMEM((GROW * COLROWS, LANES), F32)],
         compiler_params=pltpu.CompilerParams(vmem_limit_bytes=14 << 20),
@@ -334,9 +340,12 @@
     )(place, *cols)
 
 
+PIECES = 7
+
+
 def away_kernel(weighted, *refs):
-    pieces = refs[:5]
-    away_out, turned_out, rows, sems = refs[5:]
+    pieces = refs[:PIECES]
+    away_out, turned_out, rows, sems = refs[PIECES:]
     for copy in fetch(pieces, rows, sems):
         copy.wait()
 
@@ -358,9 +367,9 @@
             jax.ShapeDtypeStruct((ROW, NP), BF16),
             jax.ShapeDtypeStruct((ROW, PANEL), BF16),
         ),
-        in_specs=[vmem] + [pl.BlockSpec(memory_space=pl.ANY)] * 5,
+        in_specs=[vmem] + [pl.BlockSpec(memory_space=pl.ANY)] * PIECES,
         out_specs=(vmem, vmem),
-        scratch_shapes=[VMEM((PANEL, ROW), BF16), pltpu.SemaphoreType.DMA((5,))],
+        scratch_shapes=[VMEM((PANEL, ROW), BF16), pltpu.SemaphoreType.DMA((PIECES,))],
         compiler_params=pltpu.CompilerParams(vmem_limit_bytes=20 << 20),
         interpret=interpret,
         name="away",
@@ -403,12 +412,20 @@
     return lax.ppermute(array, PLANE, pairs)
 
 
-def along(array, up_by, down_by):
+ALL = ("band", "grow", "gcol_0", "gcol_1")
+
+
+def along(array, steps):
     pairs = []
-    for band, step in ((0, up_by), (1, -down_by if down_by is not None else None)):
-        if step is not None:
-            pairs += [(band * GROW + z, band * GROW + (z + step) % GROW) for z in range(GROW)]
-    return lax.ppermute(array, ("band", "grow"), pairs)
+    for band in range(2):
+        for plane in range(GCOL):
+            step = steps((band == 0) == (plane < 8), band)
+            if step is None:
+                continue
+            for z in range(GROW):
+                to = (z + step) % GROW if band == 0 else (z - step) % GROW
+                pairs.append(((band * GROW + z) * GCOL + plane, (band * GROW + to) * GCOL + plane))
+    return lax.ppermute(array, ALL, pairs)
 
 
 def swap(array):
@@ -437,19 +454,26 @@
 
 
 def exchange(place, col, rows):
-    rows = [along(rows[i], i + 1, i) for i in range(4)]
+    rows = [along(rows[i], lambda f, b, i=i: i + 1 if f else i) for i in range(4)]
     col = lax.all_to_all(col, ("gcol_0", "gcol_1"), 0, 0, tiled=True)
     row = pack_call(rows)
-    ring = [col]
-    for i in range(1, 5):
-        ring.append(along(ring[-1], 1, 1 if i < 4 else None))
+    rings = []
+    for part in range(2):
+        ring = [col[part * 8 : part * 8 + 8]]
+        for i in range(1, 5):
+            ring.append(
+                along(ring[-1], lambda f, b, i=i, part=part: 1 if i < 4 or b == part else None)
+            )
+        rings += ring
     below, above, far = turned(row, 0, 1), turned(row, 0, -1), turned(row, 0, 2)
     line = jnp.concatenate([row, below, above, far], 0)
     half = line.shape[0] // 2
-    below, above = turned(line, 1, 1), turned(line, 1, -1)
-    far_a, far_b = turned(below[:half], 1, 1), turned(above[half:], 1, -1)
-    weighted_away, weighted_home = assemble_call(place, ring)
-    away, turned_rows = away_call(weighted_away, [line, below, above, far_a, far_b])
+    below_a, above_b = turned(line[:half], 1, 1), turned(line[half:], 1, -1)
+    below_b, above_a = turned(line[half:], 1, 1), turned(line[:half], 1, -1)
+    far_a, far_b = turned(below_a, 1, 1), turned(above_b, 1, -1)
+    weighted_away, weighted_home = assemble_call(place, rings)
+    pieces = [line, below_a, below_b, above_a, above_b, far_a, far_b]
+    away, turned_rows = away_call(weighted_away, pieces)
     received = swap(away)
     home = home_call(weighted_home, turned_rows)
     return -(home + received.astype(F32))[None]

time: 112 us -> 104 us (0.929)
  blocking collectives: 15.7 us -> 0 us
  starting transfers between devices: 35.7 us -> 49 us
  waiting for transfers between devices: 29.9 us -> 22.6 us
  Pallas kernels: 25.2 us -> 26.6 us
    all_to_all x1 -> x0, blocking collectives: 15.7 us -> none  [exchange(): col = lax.all_to_all(col, ('gcol_0', 'gcol_1'), 0, 0, tiled=True)]
    ppermute x7 -> x9, starting transfers between devices: 6.21 us -> 16.7 us  [turned(): return lax.ppermute(array, PLANE, pairs)]
    ppermute x7 -> x9, waiting for transfers between devices: 15.9 us -> 10.6 us  [turned(): return lax.ppermute(array, PLANE, pairs)]
    all_to_all x0 -> x1, starting transfers between devices: none -> 5.03 us  [exchange(): col = lax.all_to_all(col, ('gcol_0', 'gcol_1'), 0, 0, tiled=True)]
    ppermute x3, starting transfers between devices: 15.4 us -> 10.6 us  [swap(): return lax.ppermute(array, 'band', [(0, 1), (1, 0)])]
    ppermute x8 -> x12, starting transfers between devices: 14.1 us -> 16.8 us  [along(): return lax.ppermute(array, ALL, pairs)]
    ppermute x8 -> x12, waiting for transfers between devices: 13.6 us -> 11.6 us  [along(): return lax.ppermute(array, ALL, pairs)]
  transfers between devices with their start and end apart: 18 -> 25, of which waited for: 12 -> 13; matrix products, arithmetic and copies ran while one was open for 2% -> 2% of each run, Pallas kernels for 7% -> 7%
where the time goes in v3:
time: 104 us
  starting transfers between devices  49 us (47%)
  Pallas kernels  26.6 us (26%)
  waiting for transfers between devices  22.6 us (22%)
  other arithmetic  2.82 us (3%)
  local copies, waits for them, and re-layouts  1.64 us (2%)
    ppermute x12, starting transfers between devices, along(): return lax.ppermute(array, ALL, pairs)  16.8 us
    ppermute x9, starting transfers between devices, turned(): return lax.ppermute(array, PLANE, pairs)  16.7 us
    pallas_call x1, Pallas kernels, density_call(): pl.pallas_call(density_kernel, out_shape=[jax.ShapeDtypeStruct((N1, 2, BL...  12.6 us
    ppermute x12, waiting for transfers between devices, along(): return lax.ppermute(array, ALL, pairs)  11.6 us
    ppermute x9, waiting for transfers between devices, turned(): return lax.ppermute(array, PLANE, pairs)  10.6 us
    ppermute x3, starting transfers between devices, swap(): return lax.ppermute(array, 'band', [(0, 1), (1, 0)])  10.6 us
    pallas_call x1, Pallas kernels, away_call(): pl.pallas_call(away_kernel, out_shape=(jax.ShapeDtypeStruct((ROW, NP), BF...  6.55 us
    all_to_all x1, starting transfers between devices, exchange(): col = lax.all_to_all(col, ('gcol_0', 'gcol_1'), 0, 0, tiled=True)  5.03 us
  transfers between devices with their start and end apart: 25, of which 13 were waited for; matrix products, arithmetic and copies ran while one was open for 2% of the time, Pallas kernels for 7%

profile of v3, /device:TPU:1, one launch (start us, length us, event | category | flops | bytes accessed | tf_op | source)
XLA Modules:
  0.0 103.5 jit_solution(960025522838772203)
XLA Ops:
  0.0 3.2 %collective-permute-start.1 = (bf16[4,98304]{1,0:T(4,128)(2,1)}, bf16[4,98304]{1,0:T(4,128)(2,1)S(1)}, u32[]{:S(2)}, u32[]{:S(2)}) collective-permute-start(bf16[4,98304]{1,0:T(4,128)(2,1)} %refs_1_.1), channel_id=1, source_target_pairs={{0,128},{128,0},{1,129},{129,1},{2,130},{130,2},{3,131},{131,3},{4... | collective-permute-start | bytes 2359304 | tf_op jit(solution)/shard_map/ppermute | solution.py:432
  3.9 0.8 reshape.11
  4.6 0.1 pad_add_fusion.mine
  4.7 0.0 collective-permute-start
  4.7 0.8 reshape.12.refs_7_
  5.6 0.3 collective-permute-done.other
  5.9 0.0 collective-permute-done.1.refs_2_
  5.9 12.6 %density.1 = (bf16[16,2,64,128]{3,2,1,0:T(8,128)(2,1)}, bf16[2,120,128]{2,1,0:T(8,128)(2,1)S(1)}, bf16[2,120,128]{2,1,0:T(8,128)(2,1)S(1)}, bf16[2,120,128]{2,1,0:T(8,128)(2,1)S(1)}, bf16[2,120,128]{2,1,0:T(8,128)(2,1)S(1)}) custom-call(s32[1]{0:T(128)} %bitcast.place, s32[48]{0:T(128)S(1)} %pad_add_fusion.mine, s32[48]{0:T(128)S(1)} %collective-permute-done.other, ...), custom_call_target="tpu_custom_call" | custom-call | tf_op jit(solution)/shard_map/density/pallas_call | solution.py:194
  18.5 5.0 %all-to-all-start = ((bf16[16,2,64,128]{3,2,1,0:T(8,128)(2,1)}), bf16[16,2,64,128]{3,2,1,0:T(8,128)(2,1)S(1)}, u32[]{:S(2)}, u32[]{:S(2)}) async-start(bf16[16,2,64,128]{3,2,1,0:T(8,128)(2,1)} %get-tuple-element.14), calls=%async_computation | async-start | bytes 1048576 | tf_op jit(solution)/shard_map/all_to_all | solution.py:458
  23.6 0.7 collective-permute-start.10
  24.2 5.7 %collective-permute-start.11 = (bf16[2,120,128]{2,1,0:T(8,128)(2,1)S(1)}, bf16[2,120,128]{2,1,0:T(8,128)(2,1)S(1)}, u32[]{:S(2)}, u32[]{:S(2)}) collective-permute-start(bf16[2,120,128]{2,1,0:T(8,128)(2,1)S(1)} %get-tuple-element.18), channel_id=1, source_target_pairs={{0,32},{16,48},{32,64},{48,80},{64,96},{80,112},{96,0},{112,16},{1... | collective-permute-start | bytes 184328 | tf_op jit(solution)/shard_map/ppermute | solution.py:428
  29.9 1.1 %collective-permute-start.12 = (bf16[2,120,128]{2,1,0:T(8,128)(2,1)S(1)}, bf16[2,120,128]{2,1,0:T(8,128)(2,1)S(1)}, u32[]{:S(2)}, u32[]{:S(2)}) collective-permute-start(bf16[2,120,128]{2,1,0:T(8,128)(2,1)S(1)} %get-tuple-element.19), channel_id=1, source_target_pairs={{0,48},{16,64},{32,80},{48,96},{64,112},{80,0},{96,16},{112,32},{1... | collective-permute-start | bytes 184328 | tf_op jit(solution)/shard_map/ppermute | solution.py:428
  31.1 0.5 collective-permute-start.13
  31.6 0.0 collective-permute-done.10.refs_0_
  31.6 0.0 collective-permute-done.11.refs_1_
  31.6 2.6 %collective-permute-done.12.refs_2_ = bf16[2,120,128]{2,1,0:T(8,128)(2,1)S(1)} collective-permute-done((bf16[2,120,128]{2,1,0:T(8,128)(2,1)S(1)}, bf16[2,120,128]{2,1,0:T(8,128)(2,1)S(1)}, u32[]{:S(2)}, u32[]{:S(2)}) %collective-permute-start.12) | collective-permute-done | bytes 61472 | tf_op jit(solution)/shard_map/ppermute | solution.py:428
  34.2 2.0 %collective-permute-done.13.refs_3_ = bf16[2,120,128]{2,1,0:T(8,128)(2,1)S(1)} collective-permute-done((bf16[2,120,128]{2,1,0:T(8,128)(2,1)S(1)}, bf16[2,120,128]{2,1,0:T(8,128)(2,1)S(1)}, u32[]{:S(2)}, u32[]{:S(2)}) %collective-permute-start.13) | collective-permute-done | bytes 61472 | tf_op jit(solution)/shard_map/ppermute | solution.py:428
  36.3 0.1 pack.1
  36.3 7.5 %collective-permute-start.15 = (bf16[80,1536]{1,0:T(8,128)(2,1)S(1)}, bf16[80,1536]{1,0:T(8,128)(2,1)S(1)}, u32[]{:S(2)}, u32[]{:S(2)}) collective-permute-start(bf16[80,1536]{1,0:T(8,128)(2,1)S(1)} %pack.1), channel_id=1, source_target_pairs={{0,3},{1,0},{2,1},{3,2},{4,7},{5,4},{6,5},{7,6},{8,11},{9,8},{10,9... | collective-permute-start | bytes 737288 | tf_op jit(solution)/shard_map/ppermute | solution.py:412
  43.8 0.4 collective-permute-start.16
  44.2 0.8 collective-permute-start.14
  45.0 0.0 all-to-all-done
  45.0 0.1 collective-permute-start.6
  45.1 1.1 %collective-permute-start.2 = (bf16[8,2,64,128]{3,2,1,0:T(8,128)(2,1)S(1)}, bf16[8,2,64,128]{3,2,1,0:T(8,128)(2,1)S(1)}, u32[]{:S(2)}, u32[]{:S(2)}) collective-permute-start(bf16[8,2,64,128]{3,2,1,0:T(8,128)(2,1)S(1)} %get-tuple-element.24.refs_0_), channel_id=1, source_target_pairs={{0,16},{16,32},{32,48},{48,64},{64,80},{80,96},{96,112},{112,0},{1... | collective-permute-start | bytes 786440 | tf_op jit(solution)/shard_map/ppermute | solution.py:428
  46.2 3.4 %collective-permute-done.15 = bf16[80,1536]{1,0:T(8,128)(2,1)S(1)} collective-permute-done((bf16[80,1536]{1,0:T(8,128)(2,1)S(1)}, bf16[80,1536]{1,0:T(8,128)(2,1)S(1)}, u32[]{:S(2)}, u32[]{:S(2)}) %collective-permute-start.15) | collective-permute-done | bytes 245792 | tf_op jit(solution)/shard_map/ppermute | solution.py:412
  49.6 0.9 collective-permute-done.16
  50.5 2.7 %collective-permute-start.20 = (bf16[160,1536]{1,0:T(8,128)(2,1)S(1)}, bf16[160,1536]{1,0:T(8,128)(2,1)S(1)}, u32[]{:S(2)}, u32[]{:S(2)}) collective-permute-start(bf16[160,1536]{1,0:T(8,128)(2,1)S(1)} %constant_dynamic-update-slice_fusion), channel_id=1, source_target_pairs={{0,12},{1,13},{2,14},{3,15},{4,0},{5,1},{6,2},{7,3},{8,4},{9,5},{1... | collective-permute-start | bytes 1474568 | tf_op jit(solution)/shard_map/ppermute | solution.py:412
  53.2 0.0 collective-permute-done.6.refs_6_
  53.2 0.0 collective-permute-start.7
  53.2 0.2 collective-permute-done.2.refs_1_
  53.4 1.2 %collective-permute-start.3 = (bf16[8,2,64,128]{3,2,1,0:T(8,128)(2,1)S(1)}, bf16[8,2,64,128]{3,2,1,0:T(8,128)(2,1)S(1)}, u32[]{:S(2)}, u32[]{:S(2)}) collective-permute-start(bf16[8,2,64,128]{3,2,1,0:T(8,128)(2,1)S(1)} %collective-permute-done.2.refs_1_), channel_id=1, source_target_pairs={{0,16},{16,32},{32,48},{48,64},{64,80},{80,96},{96,112},{112,0},{1... | collective-permute-start | bytes 786440 | tf_op jit(solution)/shard_map/ppermute | solution.py:428
  54.6 0.0 collective-permute-done.14
  54.7 1.1 %collective-permute-start.17 = (bf16[160,1536]{1,0:T(8,128)(2,1)S(1)}, bf16[160,1536]{1,0:T(8,128)(2,1)S(1)}, u32[]{:S(2)}, u32[]{:S(2)}) collective-permute-start(bf16[160,1536]{1,0:T(8,128)(2,1)S(1)} %pad_maximum_fusion.1), channel_id=1, source_target_pairs={{0,4},{1,5},{2,6},{3,7},{4,8},{5,9},{6,10},{7,11},{8,12},{9,13},{1... | collective-permute-start | bytes 1474568 | tf_op jit(solution)/shard_map/ppermute | solution.py:412
  55.8 2.9 %collective-permute-done.7.refs_7_ = bf16[8,2,64,128]{3,2,1,0:T(8,128)(2,1)S(1)} collective-permute-done((bf16[8,2,64,128]{3,2,1,0:T(8,128)(2,1)S(1)}, bf16[8,2,64,128]{3,2,1,0:T(8,128)(2,1)S(1)}, u32[]{:S(2)}, u32[]{:S(2)}) %collective-permute-start.7) | collective-permute-done | bytes 262176 | tf_op jit(solution)/shard_map/ppermute | solution.py:428
  58.7 0.9 collective-permute-start.8
  59.7 1.9 %collective-permute-done.3.refs_2_ = bf16[8,2,64,128]{3,2,1,0:T(8,128)(2,1)S(1)} collective-permute-done((bf16[8,2,64,128]{3,2,1,0:T(8,128)(2,1)S(1)}, bf16[8,2,64,128]{3,2,1,0:T(8,128)(2,1)S(1)}, u32[]{:S(2)}, u32[]{:S(2)}) %collective-permute-start.3) | collective-permute-done | bytes 262176 | tf_op jit(solution)/shard_map/ppermute | solution.py:428
  61.5 0.9 collective-permute-start.4
  62.5 1.9 %collective-permute-done.8.refs_8_ = bf16[8,2,64,128]{3,2,1,0:T(8,128)(2,1)S(1)} collective-permute-done((bf16[8,2,64,128]{3,2,1,0:T(8,128)(2,1)S(1)}, bf16[8,2,64,128]{3,2,1,0:T(8,128)(2,1)S(1)}, u32[]{:S(2)}, u32[]{:S(2)}) %collective-permute-start.8) | collective-permute-done | bytes 262176 | tf_op jit(solution)/shard_map/ppermute | solution.py:428
  64.4 3.9 %collective-permute-start.9 = (bf16[8,2,64,128]{3,2,1,0:T(8,128)(2,1)S(1)}, bf16[8,2,64,128]{3,2,1,0:T(8,128)(2,1)S(1)}, u32[]{:S(2)}, u32[]{:S(2)}) collective-permute-start(bf16[8,2,64,128]{3,2,1,0:T(8,128)(2,1)S(1)} %collective-permute-done.8.refs_8_), channel_id=1, source_target_pairs={{128,240},{144,128},{160,144},{176,160},{192,176},{208,192},{224,2... | collective-permute-start | bytes 786440 | tf_op jit(solution)/shard_map/ppermute | solution.py:428
  68.3 0.1 collective-permute-start.18
  68.4 0.0 collective-permute-done.20.refs_4_
  68.4 2.7 %collective-permute-start.19 = (bf16[160,1536]{1,0:T(8,128)(2,1)S(1)}, bf16[160,1536]{1,0:T(8,128)(2,1)S(1)}, u32[]{:S(2)}, u32[]{:S(2)}) collective-permute-start(bf16[160,1536]{1,0:T(8,128)(2,1)S(1)} %pad_maximum_fusion.1), channel_id=1, source_target_pairs={{0,12},{1,13},{2,14},{3,15},{4,0},{5,1},{6,2},{7,3},{8,4},{9,5},{1... | collective-permute-start | bytes 1474568 | tf_op jit(solution)/shard_map/ppermute | solution.py:412
  71.0 0.0 collective-permute-done.17.refs_1_
  71.0 0.1 collective-permute-start.22
  71.1 0.0 collective-permute-done.4.refs_3_
  71.1 1.4 %collective-permute-start.21 = (bf16[160,1536]{1,0:T(8,128)(2,1)S(1)}, bf16[160,1536]{1,0:T(8,128)(2,1)S(1)}, u32[]{:S(2)}, u32[]{:S(2)}) collective-permute-start(bf16[160,1536]{1,0:T(8,128)(2,1)S(1)} %collective-permute-done.17.refs_1_), channel_id=1, source_target_pairs={{0,4},{1,5},{2,6},{3,7},{4,8},{5,9},{6,10},{7,11},{8,12},{9,13},{1... | collective-permute-start | bytes 1474568 | tf_op jit(solution)/shard_map/ppermute | solution.py:412
  72.5 0.0 collective-permute-done.9.refs_9_
  72.5 0.7 collective-permute-start.5
  73.2 0.1 pad_maximum_fusion.refs_0_
  73.3 0.0 collective-permute-done.5.refs_4_
  73.3 3.2 %assemble.1 = (bf16[1280,768]{1,0:T(8,128)(2,1)S(1)}, bf16[1280,768]{1,0:T(8,128)(2,1)S(1)}) custom-call(s32[1]{0:T(128)} %bitcast.place, bf16[8,2,64,128]{3,2,1,0:T(8,128)(2,1)S(1)} %get-tuple-element.24.refs_0_, bf16[8,2,64,128]{3,2,1,0:T(8,128)(2,1)S(1)} %collective-permute-done.2.refs_1_, bf16[8,2,64,128]{3,2,1,0:T(8,128)(2,1)S(1)} %collective-permute-done.3.refs_2_, ...), custom_call_target="tpu_custom_call" | custom-call | tf_op jit(solution)/shard_map/assemble/pallas_call | solution.py:331
  76.5 1.0 %collective-permute-done.18.refs_2_ = bf16[160,1536]{1,0:T(8,128)(2,1)S(1)} collective-permute-done((bf16[160,1536]{1,0:T(8,128)(2,1)S(1)}, bf16[160,1536]{1,0:T(8,128)(2,1)S(1)}, u32[]{:S(2)}, u32[]{:S(2)}) %collective-permute-start.18) | collective-permute-done | bytes 491552 | tf_op jit(solution)/shard_map/ppermute | solution.py:412
  77.5 0.0 collective-permute-done.19.refs_3_
  77.6 4.5 %collective-permute-done.22.refs_6_ = bf16[160,1536]{1,0:T(8,128)(2,1)S(1)} collective-permute-done((bf16[160,1536]{1,0:T(8,128)(2,1)S(1)}, bf16[160,1536]{1,0:T(8,128)(2,1)S(1)}, u32[]{:S(2)}, u32[]{:S(2)}) %collective-permute-start.22) | collective-permute-done | bytes 491552 | tf_op jit(solution)/shard_map/ppermute | solution.py:412
  82.1 0.7 collective-permute-done.21.refs_5_
  82.8 6.5 %away.1 = (bf16[1536,768]{1,0:T(8,128)(2,1)S(1)}, bf16[1536,1280]{1,0:T(8,128)(2,1)S(1)}) custom-call(bf16[1280,768]{1,0:T(8,128)(2,1)S(1)} %get-tuple-element.16.weighted, bf16[320,1536]{1,0:T(8,128)(2,1)S(1)} %pad_maximum_fusion.refs_0_, bf16[160,1536]{1,0:T(8,128)(2,1)S(1)} %collective-permute-done.17.refs_1_, ...), custom_call_target="tpu_custom_call" | custom-call | tf_op jit(solution)/shard_map/away/pallas_call | solution.py:364
  89.4 7.3 %collective-permute-start.23 = (bf16[1536,768]{1,0:T(8,128)(2,1)S(1)}, bf16[1536,768]{1,0:T(8,128)(2,1)S(1)}, u32[]{:S(2)}, u32[]{:S(2)}) collective-permute-start(bf16[1536,768]{1,0:T(8,128)(2,1)S(1)} %get-tuple-element.22), channel_id=1, source_target_pairs={{0,128},{128,0},{1,129},{129,1},{2,130},{130,2},{3,131},{131,3},{4... | collective-permute-start | bytes 7077896 | tf_op jit(solution)/shard_map/ppermute | solution.py:432
  96.7 4.1 %home.1 = f32[1536,768]{1,0:T(8,128)S(1)} custom-call(bf16[1280,768]{1,0:T(8,128)(2,1)S(1)} %get-tuple-element.15.weighted, bf16[1536,1280]{1,0:T(8,128)(2,1)S(1)} %get-tuple-element.21.rows), custom_call_target="tpu_custom_call" | custom-call | tf_op jit(solution)/shard_map/home/pallas_call | solution.py:390
  100.8 0.1 collective-permute-done.23
  100.9 2.6 %negate_bitcast_fusion = f32[1,1536,768]{2,1,0:T(8,128)} fusion(f32[1536,768]{1,0:T(8,128)S(1)} %home.1, bf16[1536,768]{1,0:T(8,128)(2,1)S(1)} %collective-permute-done.23), kind=kLoop, calls=%fused_computation | loop fusion | flops 3538944 | bytes 11796480 | tf_op jit(solution)/shard_map/neg | solution.py:479
  (5 shorter events, 0.1 us)
Async XLA Ops:
  0.0 5.9 %collective-permute-start.1 = (bf16[4,98304]{1,0:T(4,128)(2,1)}, bf16[4,98304]{1,0:T(4,128)(2,1)S(1)}, u32[]{:S(2)}, u32[]{:S(2)}) collective-permute-start(bf16[4,98304]{1,0:T(4,128)(2,1)} %refs_1_.1), channel_id=1, source_target_pairs={{0,128},{128,0},{1,129},{129,1},{2,130},{130,2},{3,131},{131,3},{4... | collective-permute-start | bytes 2359304 | tf_op jit(solution)/shard_map/ppermute | solution.py:432
  4.7 1.2 %collective-permute-start = (s32[48]{0:T(128)S(1)}, s32[48]{0:T(128)S(1)}, u32[]{:S(2)}, u32[]{:S(2)}) collective-permute-start(s32[48]{0:T(128)S(1)} %pad_add_fusion.mine), channel_id=1, source_target_pairs={{0,128},{128,0},{1,129},{129,1},{2,130},{130,2},{3,131},{131,3},{4... | collective-permute-start | bytes 584 | tf_op jit(solution)/shard_map/ppermute | solution.py:432
  18.5 26.5 %all-to-all-start = ((bf16[16,2,64,128]{3,2,1,0:T(8,128)(2,1)}), bf16[16,2,64,128]{3,2,1,0:T(8,128)(2,1)S(1)}, u32[]{:S(2)}, u32[]{:S(2)}) async-start(bf16[16,2,64,128]{3,2,1,0:T(8,128)(2,1)} %get-tuple-element.14), calls=%async_computation | async-start | bytes 1048576 | tf_op jit(solution)/shard_map/all_to_all | solution.py:458
  23.6 8.0 %collective-permute-start.10 = (bf16[2,120,128]{2,1,0:T(8,128)(2,1)S(1)}, bf16[2,120,128]{2,1,0:T(8,128)(2,1)S(1)}, u32[]{:S(2)}, u32[]{:S(2)}) collective-permute-start(bf16[2,120,128]{2,1,0:T(8,128)(2,1)S(1)} %get-tuple-element.17), channel_id=1, source_target_pairs={{0,16},{16,32},{32,48},{48,64},{64,80},{80,96},{96,112},{112,0},{1... | collective-permute-start | bytes 184328 | tf_op jit(solution)/shard_map/ppermute | solution.py:428
  24.2 7.3 %collective-permute-start.11 = (bf16[2,120,128]{2,1,0:T(8,128)(2,1)S(1)}, bf16[2,120,128]{2,1,0:T(8,128)(2,1)S(1)}, u32[]{:S(2)}, u32[]{:S(2)}) collective-permute-start(bf16[2,120,128]{2,1,0:T(8,128)(2,1)S(1)} %get-tuple-element.18), channel_id=1, source_target_pairs={{0,32},{16,48},{32,64},{48,80},{64,96},{80,112},{96,0},{112,16},{1... | collective-permute-start | bytes 184328 | tf_op jit(solution)/shard_map/ppermute | solution.py:428
  29.9 4.3 %collective-permute-start.12 = (bf16[2,120,128]{2,1,0:T(8,128)(2,1)S(1)}, bf16[2,120,128]{2,1,0:T(8,128)(2,1)S(1)}, u32[]{:S(2)}, u32[]{:S(2)}) collective-permute-start(bf16[2,120,128]{2,1,0:T(8,128)(2,1)S(1)} %get-tuple-element.19), channel_id=1, source_target_pairs={{0,48},{16,64},{32,80},{48,96},{64,112},{80,0},{96,16},{112,32},{1... | collective-permute-start | bytes 184328 | tf_op jit(solution)/shard_map/ppermute | solution.py:428
  31.1 5.2 %collective-permute-start.13 = (bf16[2,120,128]{2,1,0:T(8,128)(2,1)S(1)}, bf16[2,120,128]{2,1,0:T(8,128)(2,1)S(1)}, u32[]{:S(2)}, u32[]{:S(2)}) collective-permute-start(bf16[2,120,128]{2,1,0:T(8,128)(2,1)S(1)} %get-tuple-element.20), channel_id=1, source_target_pairs={{0,64},{16,80},{32,96},{48,112},{64,0},{80,16},{96,32},{112,48},{1... | collective-permute-start | bytes 184328 | tf_op jit(solution)/shard_map/ppermute | solution.py:428
  36.3 13.3 %collective-permute-start.15 = (bf16[80,1536]{1,0:T(8,128)(2,1)S(1)}, bf16[80,1536]{1,0:T(8,128)(2,1)S(1)}, u32[]{:S(2)}, u32[]{:S(2)}) collective-permute-start(bf16[80,1536]{1,0:T(8,128)(2,1)S(1)} %pack.1), channel_id=1, source_target_pairs={{0,3},{1,0},{2,1},{3,2},{4,7},{5,4},{6,5},{7,6},{8,11},{9,8},{10,9... | collective-permute-start | bytes 737288 | tf_op jit(solution)/shard_map/ppermute | solution.py:412
  43.8 6.7 %collective-permute-start.16 = (bf16[80,1536]{1,0:T(8,128)(2,1)S(1)}, bf16[80,1536]{1,0:T(8,128)(2,1)S(1)}, u32[]{:S(2)}, u32[]{:S(2)}) collective-permute-start(bf16[80,1536]{1,0:T(8,128)(2,1)S(1)} %pack.1), channel_id=1, source_target_pairs={{0,2},{1,3},{2,0},{3,1},{4,6},{5,7},{6,4},{7,5},{8,10},{9,11},{10,... | collective-permute-start | bytes 737288 | tf_op jit(solution)/shard_map/ppermute | solution.py:412
  44.2 10.4 %collective-permute-start.14 = (bf16[80,1536]{1,0:T(8,128)(2,1)S(1)}, bf16[80,1536]{1,0:T(8,128)(2,1)S(1)}, u32[]{:S(2)}, u32[]{:S(2)}) collective-permute-start(bf16[80,1536]{1,0:T(8,128)(2,1)S(1)} %pack.1), channel_id=1, source_target_pairs={{0,1},{1,2},{2,3},{3,0},{4,5},{5,6},{6,7},{7,4},{8,9},{9,10},{10,1... | collective-permute-start | bytes 737288 | tf_op jit(solution)/shard_map/ppermute | solution.py:412
  45.0 8.2 %collective-permute-start.6 = (bf16[8,2,64,128]{3,2,1,0:T(8,128)(2,1)S(1)}, bf16[8,2,64,128]{3,2,1,0:T(8,128)(2,1)S(1)}, u32[]{:S(2)}, u32[]{:S(2)}) collective-permute-start(bf16[8,2,64,128]{3,2,1,0:T(8,128)(2,1)S(1)} %get-tuple-element.23.refs_5_), channel_id=1, source_target_pairs={{0,16},{16,32},{32,48},{48,64},{64,80},{80,96},{96,112},{112,0},{1... | collective-permute-start | bytes 786440 | tf_op jit(solution)/shard_map/ppermute | solution.py:428
  45.1 8.3 %collective-permute-start.2 = (bf16[8,2,64,128]{3,2,1,0:T(8,128)(2,1)S(1)}, bf16[8,2,64,128]{3,2,1,0:T(8,128)(2,1)S(1)}, u32[]{:S(2)}, u32[]{:S(2)}) collective-permute-start(bf16[8,2,64,128]{3,2,1,0:T(8,128)(2,1)S(1)} %get-tuple-element.24.refs_0_), channel_id=1, source_target_pairs={{0,16},{16,32},{32,48},{48,64},{64,80},{80,96},{96,112},{112,0},{1... | collective-permute-start | bytes 786440 | tf_op jit(solution)/shard_map/ppermute | solution.py:428
  50.5 17.9 %collective-permute-start.20 = (bf16[160,1536]{1,0:T(8,128)(2,1)S(1)}, bf16[160,1536]{1,0:T(8,128)(2,1)S(1)}, u32[]{:S(2)}, u32[]{:S(2)}) collective-permute-start(bf16[160,1536]{1,0:T(8,128)(2,1)S(1)} %constant_dynamic-update-slice_fusion), channel_id=1, source_target_pairs={{0,12},{1,13},{2,14},{3,15},{4,0},{5,1},{6,2},{7,3},{8,4},{9,5},{1... | collective-permute-start | bytes 1474568 | tf_op jit(solution)/shard_map/ppermute | solution.py:412
  53.2 5.5 %collective-permute-start.7 = (bf16[8,2,64,128]{3,2,1,0:T(8,128)(2,1)S(1)}, bf16[8,2,64,128]{3,2,1,0:T(8,128)(2,1)S(1)}, u32[]{:S(2)}, u32[]{:S(2)}) collective-permute-start(bf16[8,2,64,128]{3,2,1,0:T(8,128)(2,1)S(1)} %collective-permute-done.6.refs_6_), channel_id=1, source_target_pairs={{0,16},{16,32},{32,48},{48,64},{64,80},{80,96},{96,112},{112,0},{1... | collective-permute-start | bytes 786440 | tf_op jit(solution)/shard_map/ppermute | solution.py:428
  53.4 8.1 %collective-permute-start.3 = (bf16[8,2,64,128]{3,2,1,0:T(8,128)(2,1)S(1)}, bf16[8,2,64,128]{3,2,1,0:T(8,128)(2,1)S(1)}, u32[]{:S(2)}, u32[]{:S(2)}) collective-permute-start(bf16[8,2,64,128]{3,2,1,0:T(8,128)(2,1)S(1)} %collective-permute-done.2.refs_1_), channel_id=1, source_target_pairs={{0,16},{16,32},{32,48},{48,64},{64,80},{80,96},{96,112},{112,0},{1... | collective-permute-start | bytes 786440 | tf_op jit(solution)/shard_map/ppermute | solution.py:428
  54.7 16.4 %collective-permute-start.17 = (bf16[160,1536]{1,0:T(8,128)(2,1)S(1)}, bf16[160,1536]{1,0:T(8,128)(2,1)S(1)}, u32[]{:S(2)}, u32[]{:S(2)}) collective-permute-start(bf16[160,1536]{1,0:T(8,128)(2,1)S(1)} %pad_maximum_fusion.1), channel_id=1, source_target_pairs={{0,4},{1,5},{2,6},{3,7},{4,8},{5,9},{6,10},{7,11},{8,12},{9,13},{1... | collective-permute-start | bytes 1474568 | tf_op jit(solution)/shard_map/ppermute | solution.py:412
  58.7 5.6 %collective-permute-start.8 = (bf16[8,2,64,128]{3,2,1,0:T(8,128)(2,1)S(1)}, bf16[8,2,64,128]{3,2,1,0:T(8,128)(2,1)S(1)}, u32[]{:S(2)}, u32[]{:S(2)}) collective-permute-start(bf16[8,2,64,128]{3,2,1,0:T(8,128)(2,1)S(1)} %collective-permute-done.7.refs_7_), channel_id=1, source_target_pairs={{0,16},{16,32},{32,48},{48,64},{64,80},{80,96},{96,112},{112,0},{1... | collective-permute-start | bytes 786440 | tf_op jit(solution)/shard_map/ppermute | solution.py:428
  61.5 9.6 %collective-permute-start.4 = (bf16[8,2,64,128]{3,2,1,0:T(8,128)(2,1)S(1)}, bf16[8,2,64,128]{3,2,1,0:T(8,128)(2,1)S(1)}, u32[]{:S(2)}, u32[]{:S(2)}) collective-permute-start(bf16[8,2,64,128]{3,2,1,0:T(8,128)(2,1)S(1)} %collective-permute-done.3.refs_2_), channel_id=1, source_target_pairs={{0,16},{16,32},{32,48},{48,64},{64,80},{80,96},{96,112},{112,0},{1... | collective-permute-start | bytes 786440 | tf_op jit(solution)/shard_map/ppermute | solution.py:428
  64.4 8.2 %collective-permute-start.9 = (bf16[8,2,64,128]{3,2,1,0:T(8,128)(2,1)S(1)}, bf16[8,2,64,128]{3,2,1,0:T(8,128)(2,1)S(1)}, u32[]{:S(2)}, u32[]{:S(2)}) collective-permute-start(bf16[8,2,64,128]{3,2,1,0:T(8,128)(2,1)S(1)} %collective-permute-done.8.refs_8_), channel_id=1, source_target_pairs={{128,240},{144,128},{160,144},{176,160},{192,176},{208,192},{224,2... | collective-permute-start | bytes 786440 | tf_op jit(solution)/shard_map/ppermute | solution.py:428
  68.3 9.3 %collective-permute-start.18 = (bf16[160,1536]{1,0:T(8,128)(2,1)S(1)}, bf16[160,1536]{1,0:T(8,128)(2,1)S(1)}, u32[]{:S(2)}, u32[]{:S(2)}) collective-permute-start(bf16[160,1536]{1,0:T(8,128)(2,1)S(1)} %constant_dynamic-update-slice_fusion), channel_id=1, source_target_pairs={{0,4},{1,5},{2,6},{3,7},{4,8},{5,9},{6,10},{7,11},{8,12},{9,13},{1... | collective-permute-start | bytes 1474568 | tf_op jit(solution)/shard_map/ppermute | solution.py:412
  68.4 9.2 %collective-permute-start.19 = (bf16[160,1536]{1,0:T(8,128)(2,1)S(1)}, bf16[160,1536]{1,0:T(8,128)(2,1)S(1)}, u32[]{:S(2)}, u32[]{:S(2)}) collective-permute-start(bf16[160,1536]{1,0:T(8,128)(2,1)S(1)} %pad_maximum_fusion.1), channel_id=1, source_target_pairs={{0,12},{1,13},{2,14},{3,15},{4,0},{5,1},{6,2},{7,3},{8,4},{9,5},{1... | collective-permute-start | bytes 1474568 | tf_op jit(solution)/shard_map/ppermute | solution.py:412
  71.0 11.0 %collective-permute-start.22 = (bf16[160,1536]{1,0:T(8,128)(2,1)S(1)}, bf16[160,1536]{1,0:T(8,128)(2,1)S(1)}, u32[]{:S(2)}, u32[]{:S(2)}) collective-permute-start(bf16[160,1536]{1,0:T(8,128)(2,1)S(1)} %collective-permute-done.20.refs_4_), channel_id=1, source_target_pairs={{0,12},{1,13},{2,14},{3,15},{4,0},{5,1},{6,2},{7,3},{8,4},{9,5},{1... | collective-permute-start | bytes 1474568 | tf_op jit(solution)/shard_map/ppermute | solution.py:412
  71.1 11.7 %collective-permute-start.21 = (bf16[160,1536]{1,0:T(8,128)(2,1)S(1)}, bf16[160,1536]{1,0:T(8,128)(2,1)S(1)}, u32[]{:S(2)}, u32[]{:S(2)}) collective-permute-start(bf16[160,1536]{1,0:T(8,128)(2,1)S(1)} %collective-permute-done.17.refs_1_), channel_id=1, source_target_pairs={{0,4},{1,5},{2,6},{3,7},{4,8},{5,9},{6,10},{7,11},{8,12},{9,13},{1... | collective-permute-start | bytes 1474568 | tf_op jit(solution)/shard_map/ppermute | solution.py:412
  72.5 0.8 collective-permute-start.5
  89.4 11.5 %collective-permute-start.23 = (bf16[1536,768]{1,0:T(8,128)(2,1)S(1)}, bf16[1536,768]{1,0:T(8,128)(2,1)S(1)}, u32[]{:S(2)}, u32[]{:S(2)}) collective-permute-start(bf16[1536,768]{1,0:T(8,128)(2,1)S(1)} %get-tuple-element.22), channel_id=1, source_target_pairs={{0,128},{128,0},{1,129},{129,1},{2,130},{130,2},{3,131},{131,3},{4... | collective-permute-start | bytes 7077896 | tf_op jit(solution)/shard_map/ppermute | solution.py:432
